TPU v7x, 32 devices: a whole 2x2x4 slice. The times are simulated.
32 devices in a mesh: dp: 4 (over x, core), seq: 4 (over z), tensor: 2 (over y).
Axes of the slice: x: 2, y: 2, z: 4, core: 2. Of those that a mesh axis runs over, the one named last changes fastest.
Arguments:
- queries: bfloat16 [4, 2048, 1024], P('dp', 'seq', 'tensor'), may hold values from -6 to 6
- key_vectors: bfloat16 [4, 2048, 1024], P('dp', 'seq', 'tensor'), may hold values from -6 to 6
- value_vectors: bfloat16 [4, 2048, 1024], P('dp', 'seq', 'tensor'), may hold values from -6 to 6
- log_decay: float32 [4, 8, 2048], P('dp', 'tensor'), may hold values from -0.75 to 0
- w_out: bfloat16 [1024, 3072], P('tensor'), may hold values from -0.1875 to 0.1875
- grad_out: bfloat16 [4, 2048, 3072], P('dp', 'seq', 'tensor'), may hold values from -6 to 6
Outputs:
- grad_queries: bfloat16 [4, 2048, 1024], P('dp', 'seq', 'tensor')
- grad_keys: bfloat16 [4, 2048, 1024], P('dp', 'seq', 'tensor')
- grad_values: bfloat16 [4, 2048, 1024], P('dp', 'seq', 'tensor')
- grad_w_t: float32 [3072, 1024], P(('dp', 'seq'), 'tensor')
All inputs are finite; a program needn't handle non-finite values.
Results may differ from a plain program's by a relative error of at most 0.015.
Values may be sent and summed in bfloat16 or wider, within the bound.
No kernel may reach another device: no remote copies, remote signals or barrier semaphores. Data moves between devices by JAX's collectives and lax.ppermute only.
A program may use at most 64 MiB of HBM per device.

v0:
```python
import functools
import math

import jax
import jax.numpy as jnp
from jax import lax
from jax.experimental import pallas as pl
from jax.experimental.pallas import tpu as pltpu
from jax.sharding import PartitionSpec as P


F32 = jnp.float32
BF16 = jnp.bfloat16
TILE = 256
GRANT = 24 * 1024 * 1024


def dot_nn(a, b):
    return lax.dot_general(a, b, (((1,), (0,)), ((), ())), preferred_element_type=F32)


def dot_nt(a, b):
    return lax.dot_general(a, b, (((1,), (1,)), ((), ())), preferred_element_type=F32)


def dot_tn(a, b):
    return lax.dot_general(a, b, (((0,), (0,)), ((), ())), preferred_element_type=F32)


def call(body, outs, args, scalars=None, scratch=(), near=True):
    count = 0 if scalars is None else 1
    whole = pl.BlockSpec(memory_space=pltpu.VMEM)
    given = whole if near else pl.BlockSpec(memory_space=pltpu.HBM)
    spec = pltpu.PrefetchScalarGridSpec(
        num_scalar_prefetch=count,
        in_specs=[given] * len(args),
        out_specs=[whole] * len(outs),
        scratch_shapes=list(scratch),
    )
    prefix = () if scalars is None else (scalars,)
    args = [pltpu.with_memory_space_constraint(x, pltpu.VMEM if near else pltpu.HBM) for x in args]
    limit = pltpu.CompilerParams(vmem_limit_bytes=GRANT)
    return pl.pallas_call(body, out_shape=list(outs), grid_spec=spec, compiler_params=limit)(*prefix, *args)


def after(value, *others):
    return lax.optimization_barrier((value, *others))[0]


def shape(dims, kind):
    return pltpu.VMEM(dims, kind)


def final(dims, kind):
    return jax.ShapeDtypeStruct(dims, kind)


def running_sum(values):
    length = values.shape[1]
    position = lax.broadcasted_iota(jnp.int32, values.shape, 1)
    step = 1
    while step < length:
        values = values + jnp.where(position >= step, pltpu.roll(values, step, 1), 0.0)
        step *= 2
    return values


def span_decay(decay_ref, start, stop):
    values = decay_ref[...]
    position = lax.broadcasted_iota(jnp.int32, values.shape, 1)
    inside = (position >= start) & (position < stop)
    return jnp.exp(jnp.sum(jnp.where(inside, values, 0.0), axis=1, keepdims=True))


def states_kernel(place, decay_in, query_in, key_in, value_in, *refs, heads):
    outs, (semaphores,) = refs[:-1], refs[-1:]
    state_ref, row_ref, column_ref, decay_ref, query_ref, key_ref, value_ref = outs
    pairs = ((decay_in, decay_ref), (key_in, key_ref), (value_in, value_ref), (query_in, query_ref))
    copies = [pltpu.make_async_copy(*pair, semaphores.at[n]) for n, pair in enumerate(pairs)]
    for copy in copies:
        copy.start()
    rows = key_ref.shape[0]
    width = key_ref.shape[1] // heads
    copies[0].wait()
    local = decay_ref[:, pl.ds(pl.multiple_of(place[0] * rows, 128), rows)]
    tall = row_ref.shape[0]
    local = jnp.concatenate([local] * pl.cdiv(tall, heads), axis=0)[:tall]
    cumulative = running_sum(local)
    columns = cumulative.T
    row_ref[...] = cumulative
    column_ref[...] = columns
    copies[1].wait()
    copies[2].wait()
    for h in range(heads):
        at = slice(h * width, (h + 1) * width)
        to_end = jnp.exp(cumulative[h : h + 1, rows - 1 : rows] - columns[:, h : h + 1])
        scaled = (key_ref[:, at].astype(F32) * to_end).astype(BF16)
        state_ref[h] = dot_tn(scaled, value_ref[:, at]).astype(BF16)
    copies[3].wait()


def tiles(rows):
    return [(i, j) for i in range(rows // TILE) for j in range(i + 1)]


def tile_decay(row_ref, column_ref, h, i, j):
    spread = column_ref[i * TILE : (i + 1) * TILE, h : h + 1] - row_ref[h : h + 1, j * TILE : (j + 1) * TILE]
    if i != j:
        return jnp.exp(spread)
    later = lax.broadcasted_iota(jnp.int32, (TILE, TILE), 0)
    earlier = lax.broadcasted_iota(jnp.int32, (TILE, TILE), 1)
    lower = later >= earlier
    return jnp.where(lower, jnp.exp(jnp.where(lower, spread, 0.0)), 0.0)


def weights_kernel(query_ref, key_ref, value_ref, row_ref, column_ref, weight_ref, within_ref, *, heads):
    rows = key_ref.shape[0]
    width = key_ref.shape[1] // heads
    for h in range(heads):
        at = slice(h * width, (h + 1) * width)
        sums = {}
        for n, (i, j) in enumerate(tiles(rows)):
            ti, tj = slice(i * TILE, (i + 1) * TILE), slice(j * TILE, (j + 1) * TILE)
            scores = dot_nt(query_ref[ti, at], key_ref[tj, at])
            weight = (scores * tile_decay(row_ref, column_ref, h, i, j) * (1.0 / width)).astype(BF16)
            weight_ref[h, n] = weight
            term = dot_nn(weight, value_ref[tj, at])
            sums[i] = term if i not in sums else sums[i] + term
        for i, total in sums.items():
            within_ref[i * TILE : (i + 1) * TILE, at] = total


def gather_states(decay_ref, pieces, place, rows, forward):
    factors = []
    for k in range(2, len(pieces) + 1):
        start = (place - k + 1) * rows if forward else (place + 1) * rows
        stop = place * rows if forward else (place + k) * rows
        factors.append(span_decay(decay_ref, start, stop))

    def state(h):
        total = pieces[0][h].astype(F32)
        for factor, piece in zip(factors, pieces[1:], strict=True):
            total = total + factor[h : h + 1] * piece[h].astype(F32)
        return total.astype(BF16)

    return state


def attend(place, decay_ref, query_ref, within_ref, column_ref, pieces, attn_ref, carried_ref, heads):
    rows = query_ref.shape[0]
    width = query_ref.shape[1] // heads
    state = gather_states(decay_ref, pieces, place[0], rows, True)
    for h in range(heads):
        at = slice(h * width, (h + 1) * width)
        carried = state(h)
        carried_ref[h] = carried
        scaled = query_ref[:, at].astype(F32) * (jnp.exp(column_ref[:, h : h + 1]) * (1.0 / width))
        attn_ref[:, at] = (within_ref[:, at] + dot_nn(scaled.astype(BF16), carried)).astype(BF16)


def project(place, grad_ref, attn_ref, send_ref, keep_ref, scale):
    half = keep_ref.shape[0]
    for core, into in ((1 - place[1], send_ref), (place[1], keep_ref)):
        at = pl.ds(pl.multiple_of(core * half, 128), half)
        into[...] = (dot_tn(grad_ref[:, at], attn_ref[...]) * scale).astype(BF16)


def attention_kernel(place, decay_ref, query_ref, within_ref, column_ref, *refs, heads):
    *pieces, attn_ref, carried_ref = refs
    attend(place, decay_ref, query_ref, within_ref, column_ref, pieces, attn_ref, carried_ref, heads)


def attention_project_kernel(place, decay_ref, query_ref, within_ref, column_ref, grad_ref, *refs, heads, scale):
    *pieces, attn_ref, carried_ref, send_ref, keep_ref = refs
    attend(place, decay_ref, query_ref, within_ref, column_ref, pieces, attn_ref, carried_ref, heads)
    project(place, grad_ref, attn_ref, send_ref, keep_ref, scale)


def projection_kernel(place, grad_ref, attn_ref, send_ref, keep_ref, *, scale):
    project(place, grad_ref, attn_ref, send_ref, keep_ref, scale)


def half_columns(out_ref, index, count):
    return out_ref[:, pl.ds(pl.multiple_of(index * count, 128), count)]


def grad_attn_half_kernel(place, grad_ref, out_ref, total_ref):
    total_ref[...] = dot_nt(grad_ref[...], half_columns(out_ref, place[3], grad_ref.shape[1]))


def grad_attn_kernel(place, grad_ref, out_ref, query_ref, column_ref, *refs, heads):
    *halves, grad_attn_ref, back_ref = refs
    width = query_ref.shape[1] // heads
    if halves:
        total = halves[0][...] + dot_nt(grad_ref[...], half_columns(out_ref, 1 - place[3], grad_ref.shape[1]))
    else:
        total = dot_nt(grad_ref[...], out_ref[...])
    total = total.astype(BF16)
    grad_attn_ref[...] = total
    for h in range(heads):
        at = slice(h * width, (h + 1) * width)
        scaled = query_ref[:, at].astype(F32) * (jnp.exp(column_ref[:, h : h + 1]) * (1.0 / width))
        back_ref[h] = dot_tn(scaled.astype(BF16), total[:, at]).astype(BF16)


def inner_kernel(
    query_ref, key_ref, value_ref, grad_ref, row_ref, column_ref, weight_ref, carried_ref, dq_ref, dk_ref, dv_ref, *, heads
):
    rows = key_ref.shape[0]
    width = key_ref.shape[1] // heads
    inverse = 1.0 / width
    for h in range(heads):
        at = slice(h * width, (h + 1) * width)
        dq, dk, dv = {}, {}, {}

        def add(store, index, term):
            store[index] = term if index not in store else store[index] + term

        for n, (i, j) in enumerate(tiles(rows)):
            ti, tj = slice(i * TILE, (i + 1) * TILE), slice(j * TILE, (j + 1) * TILE)
            scores = dot_nt(grad_ref[ti, at], value_ref[tj, at])
            weight = (scores * tile_decay(row_ref, column_ref, h, i, j) * inverse).astype(BF16)
            add(dq, i, dot_nn(weight, key_ref[tj, at]))
            add(dk, j, dot_tn(weight, query_ref[ti, at]))
            add(dv, j, dot_tn(weight_ref[h, n], grad_ref[ti, at]))
        for i in range(rows // TILE):
            ti = slice(i * TILE, (i + 1) * TILE)
            scaled = grad_ref[ti, at].astype(F32) * (jnp.exp(column_ref[ti, h : h + 1]) * inverse)
            dq_ref[ti, at] = (dq[i] + dot_nt(scaled.astype(BF16), carried_ref[h])).astype(BF16)
            dk_ref[ti, at] = dk[i]
            dv_ref[ti, at] = dv[i]


def outer_kernel(place, decay_ref, key_ref, value_ref, row_ref, column_ref, inner_k_ref, inner_v_ref, *refs, heads):
    *pieces, dk_ref, dv_ref = refs
    rows = key_ref.shape[0]
    width = key_ref.shape[1] // heads
    state = gather_states(decay_ref, pieces, place[0], rows, False)
    for h in range(heads):
        at = slice(h * width, (h + 1) * width)
        back = state(h)
        to_end = jnp.exp(row_ref[h : h + 1, rows - 1 : rows] - column_ref[:, h : h + 1])
        values = (value_ref[:, at].astype(F32) * to_end).astype(BF16)
        keys = (key_ref[:, at].astype(F32) * to_end).astype(BF16)
        dk_ref[:, at] = (inner_k_ref[:, at] + dot_nt(values, back)).astype(BF16)
        dv_ref[:, at] = (inner_v_ref[:, at] + dot_nn(keys, back)).astype(BF16)


def pieces_kernel(place, mine_ref, other_ref, keep_ref, send_ref):
    rows = keep_ref.shape[1]
    for n in range(4):
        owner = place[0] ^ (2, 0, 3, 1)[n]
        at = pl.ds(pl.multiple_of(owner * rows, 16), rows)
        total = mine_ref[at, :].astype(F32) + other_ref[at, :].astype(F32)
        if n < 2:
            keep_ref[n] = total
        else:
            send_ref[n - 2] = total.astype(BF16)


def halve_kernel(mine_ref, other_ref, keep_ref, send_ref):
    send_ref[...] = (mine_ref[0] + other_ref[0].astype(F32)).astype(BF16)
    keep_ref[...] = mine_ref[1] + other_ref[1].astype(F32)


def finish_kernel(place, own_ref, own_other_ref, far_ref, far_other_ref, keep_ref, send_ref):
    first = own_ref[...] + own_other_ref[...].astype(F32)
    second = far_ref[...] + far_other_ref[...].astype(F32)
    mine = place[2] == place[3]
    send_ref[...] = jnp.where(mine, second, first).astype(BF16)
    keep_ref[...] = jnp.where(mine, first, second)


def shift_up(value, count):
    return [lax.ppermute(value, "seq", [(i, i + k) for i in range(count - k)]) for k in range(1, count)]


def shift_down(value, count):
    return [lax.ppermute(value, "seq", [(i, i - k) for i in range(k, count)]) for k in range(1, count)]


def swap(value, axis, bit):
    return lax.ppermute(value, axis, [(i, i ^ bit) for i in range(lax.axis_size(axis))])


def paired_mesh(dp_count, seq_count, tensor_count):
    return tensor_count == 2 and dp_count == 2 * tensor_count and seq_count == 4


def local(queries, key_vectors, value_vectors, log_decay, w_out, grad_out):
    micro, rows, features = queries.shape
    heads = log_decay.shape[1]
    width = features // heads
    dp_count, seq_count, tensor_count = (lax.axis_size(n) for n in ("dp", "seq", "tensor"))
    seq_index, dp_index, tensor_index = (lax.axis_index(n) for n in ("seq", "dp", "tensor"))
    scale = 1.0 / math.sqrt(micro * dp_count * rows * seq_count)
    query, key, value = queries[0], key_vectors[0], value_vectors[0]
    decay, grad = log_decay[0], grad_out[0]
    columns = grad.shape[1]
    paired = paired_mesh(dp_count, seq_count, tensor_count)
    place = jnp.stack([seq_index, dp_index % 2, dp_index // 2, tensor_index]).astype(jnp.int32)
    tall = -(-heads // 8) * 8
    state_shape = shape((heads, width, width), BF16)
    token_f32, token_bf16 = shape((rows, features), F32), shape((rows, features), BF16)

    if paired:
        other = swap(grad, "tensor", 1)
    else:
        other = lax.all_gather(grad, "tensor", axis=1, tiled=True)

    state, row, column, decay, query, key, value = call(
        functools.partial(states_kernel, heads=heads),
        [state_shape, shape((tall, rows), F32), shape((rows, tall), F32), shape(decay.shape, F32)] + [token_bf16] * 3,
        [decay, query, key, value],
        place,
        [pltpu.SemaphoreType.DMA((4,))],
        near=False,
    )
    received = shift_up(state, seq_count)
    weight, within = call(
        functools.partial(weights_kernel, heads=heads),
        [shape((heads, len(tiles(rows)), TILE, TILE), BF16), token_f32],
        [query, key, value, row, column],
    )
    attend_args = [decay, query, within, column]

    if paired:
        dest = columns // 2
        piece = dest // seq_count
        parts = [shape((dest, features), BF16)] * 2

        quarter = (piece, features)

        def spread(send, keep, *behind):
            came = swap(send, "dp", 1)
            stay, go = call(
                pieces_kernel,
                [shape((2, *quarter), F32), shape((2, *quarter), BF16)],
                [after(keep, *behind), came],
                place,
            )
            return stay, swap(go, "seq", 1)

        def halve(stay, came, *behind):
            stay, go = call(halve_kernel, [shape(quarter, F32), shape(quarter, BF16)], [after(stay, *behind), came])
            return stay, swap(go, "seq", 2)

        attn, carried, send, keep = call(
            functools.partial(attention_project_kernel, heads=heads, scale=scale),
            [token_bf16, state_shape, *parts],
            [*attend_args, grad, *received],
            place,
        )
        own_stay, own_came = spread(send, keep)
        (half,) = call(grad_attn_half_kernel, [token_f32], [grad, after(w_out, own_stay)], place)
        send, keep_far = call(
            functools.partial(projection_kernel, scale=scale), parts, [other, after(attn, half)], place
        )
        own_stay, own_came = halve(own_stay, own_came, keep_far)
        last = (half,)
    else:
        attn, carried = call(
            functools.partial(attention_kernel, heads=heads),
            [token_bf16, state_shape],
            [*attend_args, *received],
            place,
        )
        partial = (dot_tn(other, attn) * scale).astype(BF16)
        grad_w = lax.psum_scatter(partial, ("dp", "seq"), scatter_dimension=0, tiled=True).astype(F32)
        last, keep = (), attn

    if paired:
        keep = own_stay
    grad_attn, back = call(
        functools.partial(grad_attn_kernel, heads=heads),
        [token_bf16, state_shape],
        [other, w_out, after(query, keep), column, *last],
        place,
    )
    returned = shift_down(back, seq_count)
    if paired:
        far_stay, far_came = spread(send, keep_far, back)
        grad_attn = after(grad_attn, far_stay)
    grad_queries, inner_keys, inner_values = call(
        functools.partial(inner_kernel, heads=heads),
        [final((rows, features), BF16), token_f32, token_f32],
        [query, key, value, grad_attn, row, column, weight, carried],
    )
    if paired:
        far_stay, far_came = halve(far_stay, far_came, inner_keys)
        inner_keys = after(inner_keys, far_stay)
    grad_keys, grad_values = call(
        functools.partial(outer_kernel, heads=heads),
        [final((rows, features), BF16)] * 2,
        [decay, key, value, row, column, inner_keys, inner_values, *returned],
        place,
    )
    if paired:
        keep, send = call(
            finish_kernel,
            [shape(quarter, F32), shape(quarter, BF16)],
            [after(own_stay, grad_keys), own_came, far_stay, far_came],
            place,
        )
        grad_w = keep + swap(send, "dp", 2).astype(F32)
    return grad_queries[None], grad_keys[None], grad_values[None], grad_w


def solution(mesh):
    tokens = P("dp", "seq", "tensor")
    in_specs = (tokens, tokens, tokens, P("dp", "tensor", None), P("tensor", None), tokens)
    out_specs = (tokens, tokens, tokens, P(("dp", "seq"), "tensor"))

    step = jax.shard_map(local, mesh=mesh, in_specs=in_specs, out_specs=out_specs, check_vma=False)
    if not paired_mesh(*(mesh.shape[axis] for axis in ("dp", "seq", "tensor"))):
        return step

    return step
```

profile of v0, /device:TPU:0, one launch (start us, length us, event | category | flops | bytes accessed | tf_op | source)
XLA Modules:
  0.0 99.4 jit_solution(803650010888116170)
XLA Ops:
  0.6 3.1 %collective-permute-start = (bf16[512,1536]{1,0:T(8,128)(2,1)}, bf16[512,1536]{1,0:T(8,128)(2,1)S(1)}, u32[]{:S(2)}, u32[]{:S(2)}) collective-permute-start(bf16[512,1536]{1,0:T(8,128)(2,1)} %bitcast.12), channel_id=1, source_target_pairs={{0,1},{1,0},{2,3},{3,2},{4,5},{5,4},{6,7},{7,6},{8,9},{9,8},{10,11... | collective-permute-start | bytes 4718600 | tf_op jit(solution)/shard_map/ppermute | solution.py:283
  3.8 3.1 %shard_map.93 = (bf16[4,128,128]{2,1,0:T(8,128)(2,1)S(1)}, f32[8,512]{1,0:T(8,128)S(1)}, f32[512,8]{1,0:T(8,128)S(1)}, f32[4,2048]{1,0:T(4,128)S(1)}, bf16[512,5...) custom-call(s32[4]{0:T(128)S(1)} %pad_add_fusion.place, f32[4,2048]{1,0:T(4,128)} %bitcast.18, ...), custom_call_target="tpu_custom_call" | custom-call | tf_op jit(solution)/shard_map/pallas_call | solution.py:43
  6.9 5.5 %collective-permute-start.3 = (bf16[4,128,128]{2,1,0:T(8,128)(2,1)S(1)}, bf16[4,128,128]{2,1,0:T(8,128)(2,1)S(1)}, u32[]{:S(2)}, u32[]{:S(2)}) collective-permute-start(bf16[4,128,128]{2,1,0:T(8,128)(2,1)S(1)} %get-tuple-element.52), channel_id=1, source_target_pairs={{0,6},{1,7},{8,14},{9,15},{16,22},{17,23},{24,30},{25,31}} | collective-permute-start | bytes 393224 | tf_op jit(solution)/shard_map/ppermute | solution.py:275
  13.7 2.5 %collective-permute-start.1 = (bf16[4,128,128]{2,1,0:T(8,128)(2,1)S(1)}, bf16[4,128,128]{2,1,0:T(8,128)(2,1)S(1)}, u32[]{:S(2)}, u32[]{:S(2)}) collective-permute-start(bf16[4,128,128]{2,1,0:T(8,128)(2,1)S(1)} %get-tuple-element.52), channel_id=1, source_target_pairs={{0,2},{2,4},{4,6},{1,3},{3,5},{5,7},{8,10},{10,12},{12,14},{9,11},... | collective-permute-start | bytes 393224 | tf_op jit(solution)/shard_map/ppermute | solution.py:275
  16.2 1.6 %shard_map.94 = (bf16[4,3,256,256]{3,2,1,0:T(8,128)(2,1)S(1)}, f32[512,512]{1,0:T(8,128)S(1)}) custom-call(bf16[512,512]{1,0:T(8,128)(2,1)S(1)} %get-tuple-element.63.query_ref, bf16[512,512]{1,0:T(8,128)(2,1)S(1)} %get-tuple-element.46.key_ref, bf16[512,512]{1,0:T(8,128)(2,1)S(1)} %get-tuple-element.47.value_ref, f32[8,512]{1,0:T(8,128)S(1)} %get-tuple-element.49.row_ref, ...), custom_call_target="tpu_custom_call" | custom-call | tf_op jit(solution)/shard_map/pallas_call | solution.py:43
  19.1 1.4 %collective-permute-done.1.refs_0_ = bf16[4,128,128]{2,1,0:T(8,128)(2,1)S(1)} collective-permute-done((bf16[4,128,128]{2,1,0:T(8,128)(2,1)S(1)}, bf16[4,128,128]{2,1,0:T(8,128)(2,1)S(1)}, u32[]{:S(2)}, u32[]{:S(2)}) %collective-permute-start.1) | collective-permute-done | bytes 131104 | tf_op jit(solution)/shard_map/ppermute | solution.py:275
  20.5 2.1 %shard_map.95 = (bf16[512,512]{1,0:T(8,128)(2,1)S(1)}, bf16[4,128,128]{2,1,0:T(8,128)(2,1)S(1)}, bf16[768,512]{1,0:T(8,128)(2,1)S(1)}, bf16[768,512]{1,0:T(8,128)(2,1)S(1)}) custom-call(s32[4]{0:T(128)S(1)} %pad_add_fusion.place, f32[4,2048]{1,0:T(4,128)S(1)} %get-tuple-element.48.decay_ref, bf16[512,512]{1,0:T(8,128)(2,1)S(1)} %get-tuple-element.63.query_ref, ...), custom_call_target="tpu_custom_call" | custom-call | tf_op jit(solution)/shard_map/pallas_call | solution.py:43
  22.7 2.3 %collective-permute-done.4.other_ref = bf16[768,512]{1,0:T(8,128)(2,1)S(1)} collective-permute-done((bf16[768,512]{1,0:T(8,128)(2,1)S(1)}, bf16[768,512]{1,0:T(8,128)(2,1)S(1)}, u32[]{:S(2)}, u32[]{:S(2)}) %collective-permute-start.4) | collective-permute-done | bytes 786464 | tf_op jit(solution)/shard_map/ppermute | solution.py:283
  25.7 1.6 %shard_map.97.refs_0_ = f32[512,512]{1,0:T(8,128)S(1)} custom-call(s32[4]{0:T(128)S(1)} %pad_add_fusion.place, bf16[512,1536]{1,0:T(8,128)(2,1)S(1)} %bitcast.14, bf16[512,3072]{1,0:T(8,128)(2,1)S(1)} %copy-done), custom_call_target="tpu_custom_call" | custom-call | tf_op jit(solution)/shard_map/pallas_call | solution.py:43
  27.2 11.1 %collective-permute-done.grad_ref = bf16[512,1536]{1,0:T(8,128)(2,1)S(1)} collective-permute-done((bf16[512,1536]{1,0:T(8,128)(2,1)}, bf16[512,1536]{1,0:T(8,128)(2,1)S(1)}, u32[]{:S(2)}, u32[]{:S(2)}) %collective-permute-start) | collective-permute-done | bytes 1572896 | tf_op jit(solution)/shard_map/ppermute | solution.py:283
  38.3 1.6 %shard_map.98 = (bf16[768,512]{1,0:T(8,128)(2,1)S(1)}, bf16[768,512]{1,0:T(8,128)(2,1)S(1)}) custom-call(s32[4]{0:T(128)S(1)} %pad_add_fusion.place, bf16[512,1536]{1,0:T(8,128)(2,1)S(1)} %collective-permute-done.grad_ref, bf16[512,512]{1,0:T(8,128)(2,1)S(1)} %get-tuple-element.58.attn_ref), custom_call_target="tpu_custom_call" | custom-call | tf_op jit(solution)/shard_map/pallas_call | solution.py:43
  39.9 1.9 %collective-permute-start.5 = (bf16[2,192,512]{2,1,0:T(8,128)(2,1)S(1)}, bf16[2,192,512]{2,1,0:T(8,128)(2,1)S(1)}, u32[]{:S(2)}, u32[]{:S(2)}) collective-permute-start(bf16[2,192,512]{2,1,0:T(8,128)(2,1)S(1)} %get-tuple-element.61), channel_id=1, source_target_pairs={{0,2},{2,0},{4,6},{6,4},{1,3},{3,1},{5,7},{7,5},{8,10},{10,8},{12,... | collective-permute-start | bytes 1179656 | tf_op jit(solution)/shard_map/ppermute | solution.py:283
  41.8 9.7 %collective-permute-done.5.other_ref = bf16[2,192,512]{2,1,0:T(8,128)(2,1)S(1)} collective-permute-done((bf16[2,192,512]{2,1,0:T(8,128)(2,1)S(1)}, bf16[2,192,512]{2,1,0:T(8,128)(2,1)S(1)}, u32[]{:S(2)}, u32[]{:S(2)}) %collective-permute-start.5) | collective-permute-done | bytes 393248 | tf_op jit(solution)/shard_map/ppermute | solution.py:283
  51.6 1.9 %shard_map.100 = (bf16[512,512]{1,0:T(8,128)(2,1)S(1)}, bf16[4,128,128]{2,1,0:T(8,128)(2,1)S(1)}) custom-call(s32[4]{0:T(128)S(1)} %pad_add_fusion.place, bf16[512,1536]{1,0:T(8,128)(2,1)S(1)} %collective-permute-done.grad_ref, bf16[512,3072]{1,0:T(8,128)(2,1)S(1)} %copy-done, bf16[512,512]{1,0:T(8,128)(2,1)S(1)} %get-tuple-element.63.query_ref, ...), custom_call_target="tpu_custom_call" | custom-call | tf_op jit(solution)/shard_map/pallas_call | solution.py:43
  54.2 1.8 %collective-permute-start.7 = (bf16[2,192,512]{2,1,0:T(8,128)(2,1)S(1)}, bf16[2,192,512]{2,1,0:T(8,128)(2,1)S(1)}, u32[]{:S(2)}, u32[]{:S(2)}) collective-permute-start(bf16[2,192,512]{2,1,0:T(8,128)(2,1)S(1)} %get-tuple-element.75), channel_id=1, source_target_pairs={{0,2},{2,0},{4,6},{6,4},{1,3},{3,1},{5,7},{7,5},{8,10},{10,8},{12,... | collective-permute-start | bytes 1179656 | tf_op jit(solution)/shard_map/ppermute | solution.py:283
  56.0 2.6 %collective-permute-start.11 = (bf16[192,512]{1,0:T(8,128)(2,1)S(1)}, bf16[192,512]{1,0:T(8,128)(2,1)S(1)}, u32[]{:S(2)}, u32[]{:S(2)}) collective-permute-start(bf16[192,512]{1,0:T(8,128)(2,1)S(1)} %get-tuple-element.82), channel_id=1, source_target_pairs={{0,4},{2,6},{4,0},{6,2},{1,5},{3,7},{5,1},{7,3},{8,12},{10,14},{12... | collective-permute-start | bytes 589832 | tf_op jit(solution)/shard_map/ppermute | solution.py:283
  58.6 4.1 %shard_map.102 = (bf16[512,512]{1,0:T(8,128)(2,1)}, f32[512,512]{1,0:T(8,128)S(1)}, f32[512,512]{1,0:T(8,128)S(1)}) custom-call(bf16[512,512]{1,0:T(8,128)(2,1)S(1)} %get-tuple-element.63.query_ref, bf16[512,512]{1,0:T(8,128)(2,1)S(1)} %get-tuple-element.46.key_ref, bf16[512,512]{1,0:T(8,128)(2,1)S(1)} %get-tuple-element.47.value_ref, ...), custom_call_target="tpu_custom_call" | custom-call | tf_op jit(solution)/shard_map/pallas_call | solution.py:43
  62.7 6.5 %collective-permute-done.7.other_ref = bf16[2,192,512]{2,1,0:T(8,128)(2,1)S(1)} collective-permute-done((bf16[2,192,512]{2,1,0:T(8,128)(2,1)S(1)}, bf16[2,192,512]{2,1,0:T(8,128)(2,1)S(1)}, u32[]{:S(2)}, u32[]{:S(2)}) %collective-permute-start.7) | collective-permute-done | bytes 393248 | tf_op jit(solution)/shard_map/ppermute | solution.py:283
  69.2 1.9 %collective-permute-start.12 = (bf16[192,512]{1,0:T(8,128)(2,1)S(1)}, bf16[192,512]{1,0:T(8,128)(2,1)S(1)}, u32[]{:S(2)}, u32[]{:S(2)}) collective-permute-start(bf16[192,512]{1,0:T(8,128)(2,1)S(1)} %get-tuple-element.83), channel_id=1, source_target_pairs={{0,4},{2,6},{4,0},{6,2},{1,5},{3,7},{5,1},{7,3},{8,12},{10,14},{12... | collective-permute-start | bytes 589832 | tf_op jit(solution)/shard_map/ppermute | solution.py:283
  75.0 6.2 %collective-permute-done.10.refs_2_ = bf16[4,128,128]{2,1,0:T(8,128)(2,1)S(1)} collective-permute-done((bf16[4,128,128]{2,1,0:T(8,128)(2,1)S(1)}, bf16[4,128,128]{2,1,0:T(8,128)(2,1)S(1)}, u32[]{:S(2)}, u32[]{:S(2)}) %collective-permute-start.10) | collective-permute-done | bytes 131104 | tf_op jit(solution)/shard_map/ppermute | solution.py:279
  81.2 8.6 %collective-permute-done.9.refs_1_ = bf16[4,128,128]{2,1,0:T(8,128)(2,1)S(1)} collective-permute-done((bf16[4,128,128]{2,1,0:T(8,128)(2,1)S(1)}, bf16[4,128,128]{2,1,0:T(8,128)(2,1)S(1)}, u32[]{:S(2)}, u32[]{:S(2)}) %collective-permute-start.9) | collective-permute-done | bytes 131104 | tf_op jit(solution)/shard_map/ppermute | solution.py:279
  89.7 2.5 %shard_map.104 = (bf16[512,512]{1,0:T(8,128)(2,1)}, bf16[512,512]{1,0:T(8,128)(2,1)}) custom-call(s32[4]{0:T(128)S(1)} %pad_add_fusion.place, f32[4,2048]{1,0:T(4,128)S(1)} %get-tuple-element.48.decay_ref, bf16[512,512]{1,0:T(8,128)(2,1)S(1)} %get-tuple-element.46.key_ref, bf16[512,512]{1,0:T(8,128)(2,1)S(1)} %get-tuple-element.47.value_ref, ...), custom_call_target="tpu_custom_call" | custom-call | tf_op jit(solution)/shard_map/pallas_call | solution.py:43
  92.9 1.6 %collective-permute-start.13 = (bf16[192,512]{1,0:T(8,128)(2,1)S(1)}, bf16[192,512]{1,0:T(8,128)(2,1)S(1)}, u32[]{:S(2)}, u32[]{:S(2)}) collective-permute-start(bf16[192,512]{1,0:T(8,128)(2,1)S(1)} %get-tuple-element.85), channel_id=1, source_target_pairs={{0,16},{8,24},{16,0},{24,8},{1,17},{9,25},{17,1},{25,9},{2,18},{10... | collective-permute-start | bytes 589832 | tf_op jit(solution)/shard_map/ppermute | solution.py:283
  94.4 4.2 %collective-permute-done.13 = bf16[192,512]{1,0:T(8,128)(2,1)S(1)} collective-permute-done((bf16[192,512]{1,0:T(8,128)(2,1)S(1)}, bf16[192,512]{1,0:T(8,128)(2,1)S(1)}, u32[]{:S(2)}, u32[]{:S(2)}) %collective-permute-start.13) | collective-permute-done | bytes 196640 | tf_op jit(solution)/shard_map/ppermute | solution.py:283
  (23 shorter events, 9.7 us)
Async XLA Ops:
  0.6 37.7 %collective-permute-start = (bf16[512,1536]{1,0:T(8,128)(2,1)}, bf16[512,1536]{1,0:T(8,128)(2,1)S(1)}, u32[]{:S(2)}, u32[]{:S(2)}) collective-permute-start(bf16[512,1536]{1,0:T(8,128)(2,1)} %bitcast.12), channel_id=1, source_target_pairs={{0,1},{1,0},{2,3},{3,2},{4,5},{5,4},{6,7},{7,6},{8,9},{9,8},{10,11... | collective-permute-start | bytes 4718600 | tf_op jit(solution)/shard_map/ppermute | solution.py:283
  3.8 16.8 %copy-start.1 = (bf16[1,512,1536]{2,1,0:T(8,128)(2,1)S(1)}, bf16[1,512,1536]{2,1,0:T(8,128)(2,1)}, u32[]{:S(2)}) copy-start(bf16[1,512,1536]{2,1,0:T(8,128)(2,1)} %param.11) | copy-start | bytes 4718596
  6.9 10.9 %collective-permute-start.3 = (bf16[4,128,128]{2,1,0:T(8,128)(2,1)S(1)}, bf16[4,128,128]{2,1,0:T(8,128)(2,1)S(1)}, u32[]{:S(2)}, u32[]{:S(2)}) collective-permute-start(bf16[4,128,128]{2,1,0:T(8,128)(2,1)S(1)} %get-tuple-element.52), channel_id=1, source_target_pairs={{0,6},{1,7},{8,14},{9,15},{16,22},{17,23},{24,30},{25,31}} | collective-permute-start | bytes 393224 | tf_op jit(solution)/shard_map/ppermute | solution.py:275
  12.4 6.7 %collective-permute-start.2 = (bf16[4,128,128]{2,1,0:T(8,128)(2,1)S(1)}, bf16[4,128,128]{2,1,0:T(8,128)(2,1)S(1)}, u32[]{:S(2)}, u32[]{:S(2)}) collective-permute-start(bf16[4,128,128]{2,1,0:T(8,128)(2,1)S(1)} %get-tuple-element.52), channel_id=1, source_target_pairs={{0,4},{2,6},{1,5},{3,7},{8,12},{10,14},{9,13},{11,15},{16,20},{18,... | collective-permute-start | bytes 393224 | tf_op jit(solution)/shard_map/ppermute | solution.py:275
  13.7 6.8 %collective-permute-start.1 = (bf16[4,128,128]{2,1,0:T(8,128)(2,1)S(1)}, bf16[4,128,128]{2,1,0:T(8,128)(2,1)S(1)}, u32[]{:S(2)}, u32[]{:S(2)}) collective-permute-start(bf16[4,128,128]{2,1,0:T(8,128)(2,1)S(1)} %get-tuple-element.52), channel_id=1, source_target_pairs={{0,2},{2,4},{4,6},{1,3},{3,5},{5,7},{8,10},{10,12},{12,14},{9,11},... | collective-permute-start | bytes 393224 | tf_op jit(solution)/shard_map/ppermute | solution.py:275
  20.5 5.1 %copy-start = (bf16[512,3072]{1,0:T(8,128)(2,1)S(1)}, bf16[512,3072]{1,0:T(8,128)(2,1)}, u32[]{:S(2)}) copy-start(bf16[512,3072]{1,0:T(8,128)(2,1)} %out_ref.2) | copy-start | bytes 9437188
  22.6 2.4 %collective-permute-start.4 = (bf16[768,512]{1,0:T(8,128)(2,1)S(1)}, bf16[768,512]{1,0:T(8,128)(2,1)S(1)}, u32[]{:S(2)}, u32[]{:S(2)}) collective-permute-start(bf16[768,512]{1,0:T(8,128)(2,1)S(1)} %get-tuple-element.54), channel_id=1, source_target_pairs={{0,8},{8,0},{16,24},{24,16},{1,9},{9,1},{17,25},{25,17},{2,10},{10... | collective-permute-start | bytes 2359304 | tf_op jit(solution)/shard_map/ppermute | solution.py:283
  39.9 13.6 %collective-permute-start.6 = (bf16[768,512]{1,0:T(8,128)(2,1)S(1)}, bf16[768,512]{1,0:T(8,128)(2,1)S(1)}, u32[]{:S(2)}, u32[]{:S(2)}) collective-permute-start(bf16[768,512]{1,0:T(8,128)(2,1)S(1)} %get-tuple-element.67), channel_id=1, source_target_pairs={{0,8},{8,0},{16,24},{24,16},{1,9},{9,1},{17,25},{25,17},{2,10},{10... | collective-permute-start | bytes 2359304 | tf_op jit(solution)/shard_map/ppermute | solution.py:283
  39.9 11.6 %collective-permute-start.5 = (bf16[2,192,512]{2,1,0:T(8,128)(2,1)S(1)}, bf16[2,192,512]{2,1,0:T(8,128)(2,1)S(1)}, u32[]{:S(2)}, u32[]{:S(2)}) collective-permute-start(bf16[2,192,512]{2,1,0:T(8,128)(2,1)S(1)} %get-tuple-element.61), channel_id=1, source_target_pairs={{0,2},{2,0},{4,6},{6,4},{1,3},{3,1},{5,7},{7,5},{8,10},{10,8},{12,... | collective-permute-start | bytes 1179656 | tf_op jit(solution)/shard_map/ppermute | solution.py:283
  54.2 14.9 %collective-permute-start.7 = (bf16[2,192,512]{2,1,0:T(8,128)(2,1)S(1)}, bf16[2,192,512]{2,1,0:T(8,128)(2,1)S(1)}, u32[]{:S(2)}, u32[]{:S(2)}) collective-permute-start(bf16[2,192,512]{2,1,0:T(8,128)(2,1)S(1)} %get-tuple-element.75), channel_id=1, source_target_pairs={{0,2},{2,0},{4,6},{6,4},{1,3},{3,1},{5,7},{7,5},{8,10},{10,8},{12,... | collective-permute-start | bytes 1179656 | tf_op jit(solution)/shard_map/ppermute | solution.py:283
  56.0 36.2 %collective-permute-start.11 = (bf16[192,512]{1,0:T(8,128)(2,1)S(1)}, bf16[192,512]{1,0:T(8,128)(2,1)S(1)}, u32[]{:S(2)}, u32[]{:S(2)}) collective-permute-start(bf16[192,512]{1,0:T(8,128)(2,1)S(1)} %get-tuple-element.82), channel_id=1, source_target_pairs={{0,4},{2,6},{4,0},{6,2},{1,5},{3,7},{5,1},{7,3},{8,12},{10,14},{12... | collective-permute-start | bytes 589832 | tf_op jit(solution)/shard_map/ppermute | solution.py:283
  69.2 23.0 %collective-permute-start.12 = (bf16[192,512]{1,0:T(8,128)(2,1)S(1)}, bf16[192,512]{1,0:T(8,128)(2,1)S(1)}, u32[]{:S(2)}, u32[]{:S(2)}) collective-permute-start(bf16[192,512]{1,0:T(8,128)(2,1)S(1)} %get-tuple-element.83), channel_id=1, source_target_pairs={{0,4},{2,6},{4,0},{6,2},{1,5},{3,7},{5,1},{7,3},{8,12},{10,14},{12... | collective-permute-start | bytes 589832 | tf_op jit(solution)/shard_map/ppermute | solution.py:283
  71.1 10.1 %collective-permute-start.10 = (bf16[4,128,128]{2,1,0:T(8,128)(2,1)S(1)}, bf16[4,128,128]{2,1,0:T(8,128)(2,1)S(1)}, u32[]{:S(2)}, u32[]{:S(2)}) collective-permute-start(bf16[4,128,128]{2,1,0:T(8,128)(2,1)S(1)} %get-tuple-element.65), channel_id=1, source_target_pairs={{6,0},{7,1},{14,8},{15,9},{22,16},{23,17},{30,24},{31,25}} | collective-permute-start | bytes 393224 | tf_op jit(solution)/shard_map/ppermute | solution.py:279
  72.4 17.4 %collective-permute-start.9 = (bf16[4,128,128]{2,1,0:T(8,128)(2,1)S(1)}, bf16[4,128,128]{2,1,0:T(8,128)(2,1)S(1)}, u32[]{:S(2)}, u32[]{:S(2)}) collective-permute-start(bf16[4,128,128]{2,1,0:T(8,128)(2,1)S(1)} %get-tuple-element.65), channel_id=1, source_target_pairs={{4,0},{6,2},{5,1},{7,3},{12,8},{14,10},{13,9},{15,11},{20,16},{22,... | collective-permute-start | bytes 393224 | tf_op jit(solution)/shard_map/ppermute | solution.py:279
  73.7 16.1 %collective-permute-start.8 = (bf16[4,128,128]{2,1,0:T(8,128)(2,1)S(1)}, bf16[4,128,128]{2,1,0:T(8,128)(2,1)S(1)}, u32[]{:S(2)}, u32[]{:S(2)}) collective-permute-start(bf16[4,128,128]{2,1,0:T(8,128)(2,1)S(1)} %get-tuple-element.65), channel_id=1, source_target_pairs={{2,0},{4,2},{6,4},{3,1},{5,3},{7,5},{10,8},{12,10},{14,12},{11,9},... | collective-permute-start | bytes 393224 | tf_op jit(solution)/shard_map/ppermute | solution.py:279
  92.9 5.7 %collective-permute-start.13 = (bf16[192,512]{1,0:T(8,128)(2,1)S(1)}, bf16[192,512]{1,0:T(8,128)(2,1)S(1)}, u32[]{:S(2)}, u32[]{:S(2)}) collective-permute-start(bf16[192,512]{1,0:T(8,128)(2,1)S(1)} %get-tuple-element.85), channel_id=1, source_target_pairs={{0,16},{8,24},{16,0},{24,8},{1,17},{9,25},{17,1},{25,9},{2,18},{10... | collective-permute-start | bytes 589832 | tf_op jit(solution)/shard_map/ppermute | solution.py:283
where the time goes:
time: 99.6 us; the launch traced here: 99.4 us
  waiting for transfers between devices  51.2 us (51%)
  starting transfers between devices  26 us (26%)
  Pallas kernels  20.5 us (21%)
    ppermute x8, waiting for transfers between devices, swap(): lax.ppermute(value, axis, [(i, i ^ bit) for i in range(lax.axis_size(axis...  33.7 us
    pallas_call x13, Pallas kernels, call(): pl.pallas_call(body, out_shape=list(outs), grid_spec=spec, compiler_param...  20.5 us
    ppermute x3, waiting for transfers between devices, shift_down(): lax.ppermute(value, 'seq', [(i, i - k) for i in range(k, count)])  14.8 us
    ppermute x8, starting transfers between devices, swap(): lax.ppermute(value, axis, [(i, i ^ bit) for i in range(lax.axis_size(axis...  12.9 us
    ppermute x3, starting transfers between devices, shift_up(): lax.ppermute(value, 'seq', [(i, i + k) for i in range(count - k)])  9.28 us
    ppermute x3, starting transfers between devices, shift_down(): lax.ppermute(value, 'seq', [(i, i - k) for i in range(k, count)])  3.86 us
    ppermute x3, waiting for transfers between devices, shift_up(): lax.ppermute(value, 'seq', [(i, i + k) for i in range(count - k)])  2.68 us
  transfers between devices with their start and end apart: 14, of which 9 were waited for; matrix products, arithmetic and copies ran while one was open for 0% of the time, Pallas kernels for 18%

commit v1 on v0

--- a/solution.py
+++ b/solution.py
@@ -73,14 +73,15 @@
 
 
 def states_kernel(place, decay_in, query_in, key_in, value_in, *refs, heads):
-    outs, (semaphores,) = refs[:-1], refs[-1:]
+    *outs, semaphores = refs
     state_ref, row_ref, column_ref, decay_ref, query_ref, key_ref, value_ref = outs
+    rows = key_ref.shape[0]
+    width = key_ref.shape[1] // heads
+    spans = [slice(h * width, (h + 1) * width) for h in range(heads)]
     pairs = ((decay_in, decay_ref), (key_in, key_ref), (value_in, value_ref), (query_in, query_ref))
     copies = [pltpu.make_async_copy(*pair, semaphores.at[n]) for n, pair in enumerate(pairs)]
     for copy in copies:
         copy.start()
-    rows = key_ref.shape[0]
-    width = key_ref.shape[1] // heads
     copies[0].wait()
     local = decay_ref[:, pl.ds(pl.multiple_of(place[0] * rows, 128), rows)]
     tall = row_ref.shape[0]
@@ -91,8 +92,7 @@
     column_ref[...] = columns
     copies[1].wait()
     copies[2].wait()
-    for h in range(heads):
-        at = slice(h * width, (h + 1) * width)
+    for h, at in enumerate(spans):
         to_end = jnp.exp(cumulative[h : h + 1, rows - 1 : rows] - columns[:, h : h + 1])
         scaled = (key_ref[:, at].astype(F32) * to_end).astype(BF16)
         state_ref[h] = dot_tn(scaled, value_ref[:, at]).astype(BF16)
@@ -203,6 +203,12 @@
         back_ref[h] = dot_tn(scaled.astype(BF16), total[:, at]).astype(BF16)
 
 
+def chain_kernel(place, decay_ref, back_ref, came_ref, chain_ref, *, rows):
+    factor = span_decay(decay_ref, place[0] * rows, (place[0] + 1) * rows)
+    for h in range(back_ref.shape[0]):
+        chain_ref[h] = (back_ref[h].astype(F32) + factor[h : h + 1] * came_ref[h].astype(F32)).astype(BF16)
+
+
 def inner_kernel(
     query_ref, key_ref, value_ref, grad_ref, row_ref, column_ref, weight_ref, carried_ref, dq_ref, dk_ref, dv_ref, *, heads
 ):
@@ -231,11 +237,21 @@
             dv_ref[ti, at] = dv[i]
 
 
-def outer_kernel(place, decay_ref, key_ref, value_ref, row_ref, column_ref, inner_k_ref, inner_v_ref, *refs, heads):
+def summed_states(pieces):
+    def state(h):
+        total = pieces[0][h]
+        for piece in pieces[1:]:
+            total = total + piece[h]
+        return total
+
+    return state
+
+
+def outer_kernel(place, decay_ref, key_ref, value_ref, row_ref, column_ref, inner_k_ref, inner_v_ref, *refs, heads, chained):
     *pieces, dk_ref, dv_ref = refs
     rows = key_ref.shape[0]
     width = key_ref.shape[1] // heads
-    state = gather_states(decay_ref, pieces, place[0], rows, False)
+    state = summed_states(pieces) if chained else gather_states(decay_ref, pieces, place[0], rows, False)
     for h in range(heads):
         at = slice(h * width, (h + 1) * width)
         back = state(h)
@@ -258,17 +274,31 @@
             send_ref[n - 2] = total.astype(BF16)
 
 
+def direct_kernel(place, mine_ref, other_ref, keep_ref, *send_refs):
+    count, rows = len(send_refs) + 1, keep_ref.shape[0]
+    for k in range(count):
+        at = pl.ds(pl.multiple_of(lax.rem(place[0] + k, count) * rows, 16), rows)
+        total = mine_ref[at, :].astype(F32) + other_ref[at, :].astype(F32)
+        if k == 0:
+            keep_ref[...] = total
+        else:
+            send_refs[k - 1][...] = total.astype(BF16)
+
+
 def halve_kernel(mine_ref, other_ref, keep_ref, send_ref):
     send_ref[...] = (mine_ref[0] + other_ref[0].astype(F32)).astype(BF16)
     keep_ref[...] = mine_ref[1] + other_ref[1].astype(F32)
 
 
-def finish_kernel(place, own_ref, own_other_ref, far_ref, far_other_ref, keep_ref, send_ref):
-    first = own_ref[...] + own_other_ref[...].astype(F32)
-    second = far_ref[...] + far_other_ref[...].astype(F32)
+def finish_kernel(place, *refs):
+    own_ref, *own_others, far_ref, far_other_ref, keep_ref, send_ref = refs
+    own = own_ref[...]
+    for ref in own_others:
+        own = own + ref[...].astype(F32)
+    far = far_ref[...] + far_other_ref[...].astype(F32)
     mine = place[2] == place[3]
-    send_ref[...] = jnp.where(mine, second, first).astype(BF16)
-    keep_ref[...] = jnp.where(mine, first, second)
+    send_ref[...] = jnp.where(mine, far, own).astype(BF16)
+    keep_ref[...] = jnp.where(mine, own, far)
 
 
 def shift_up(value, count):
@@ -351,12 +381,21 @@
             [*attend_args, grad, *received],
             place,
         )
-        own_stay, own_came = spread(send, keep)
+        came = swap(send, "dp", 1)
+        own_stay, *own_parts = call(
+            direct_kernel,
+            [shape(quarter, F32)] + [shape(quarter, BF16)] * (seq_count - 1),
+            [keep, came],
+            place,
+        )
+        own_came = [
+            lax.ppermute(part, "seq", [(i, (i + k) % seq_count) for i in range(seq_count)])
+            for k, part in enumerate(own_parts, 1)
+        ]
         (half,) = call(grad_attn_half_kernel, [token_f32], [grad, after(w_out, own_stay)], place)
         send, keep_far = call(
             functools.partial(projection_kernel, scale=scale), parts, [other, after(attn, half)], place
         )
-        own_stay, own_came = halve(own_stay, own_came, keep_far)
         last = (half,)
     else:
         attn, carried = call(
@@ -370,14 +409,18 @@
         last, keep = (), attn
 
     if paired:
-        keep = own_stay
+        keep = keep_far
     grad_attn, back = call(
         functools.partial(grad_attn_kernel, heads=heads),
         [token_bf16, state_shape],
         [other, w_out, after(query, keep), column, *last],
         place,
     )
-    returned = shift_down(back, seq_count)
+
+    def pass_back(value, stage):
+        return lax.ppermute(value, "seq", [(seq_count - stage, seq_count - 1 - stage)])
+
+    returned = [pass_back(back, 1)] if paired else shift_down(back, seq_count)
     if paired:
         far_stay, far_came = spread(send, keep_far, back)
         grad_attn = after(grad_attn, far_stay)
@@ -387,22 +430,34 @@
         [query, key, value, grad_attn, row, column, weight, carried],
     )
     if paired:
+        def chain(stage, *behind):
+            (passed,) = call(
+                functools.partial(chain_kernel, rows=rows),
+                [state_shape],
+                [decay, after(back, *behind), returned[-1]],
+                place,
+            )
+            return pass_back(passed, stage)
+
+        returned.append(chain(2, inner_keys))
         far_stay, far_came = halve(far_stay, far_came, inner_keys)
-        inner_keys = after(inner_keys, far_stay)
+        returned.append(chain(3, far_stay))
+        keep, send = call(
+            finish_kernel,
+            [shape(quarter, F32), shape(quarter, BF16)],
+            [own_stay, *own_came, far_stay, far_came],
+            place,
+        )
+        crossed = swap(send, "dp", 2)
+        inner_keys = after(inner_keys, keep)
     grad_keys, grad_values = call(
-        functools.partial(outer_kernel, heads=heads),
+        functools.partial(outer_kernel, heads=heads, chained=paired),
         [final((rows, features), BF16)] * 2,
         [decay, key, value, row, column, inner_keys, inner_values, *returned],
         place,
     )
     if paired:
-        keep, send = call(
-            finish_kernel,
-            [shape(quarter, F32), shape(quarter, BF16)],
-            [after(own_stay, grad_keys), own_came, far_stay, far_came],
-            place,
-        )
-        grad_w = keep + swap(send, "dp", 2).astype(F32)
+        grad_w = keep + crossed.astype(F32)
     return grad_queries[None], grad_keys[None], grad_values[None], grad_w
 
 

time: 99.6 us -> 88 us (0.88)
  waiting for transfers between devices: 51.2 us -> 39.9 us
  starting transfers between devices: 26 us -> 24.3 us
  Pallas kernels: 20.5 us -> 21.9 us
    ppermute x8 -> x6, waiting for transfers between devices: 33.7 us -> 22.1 us  [swap(): lax.ppermute(value, axis, [(i, i ^ bit) for i in range(lax.axis_size(axis...]
    ppermute x8 -> x6, starting transfers between devices: 12.9 us -> 6.85 us  [swap(): lax.ppermute(value, axis, [(i, i ^ bit) for i in range(lax.axis_size(axis...]
    ppermute x3 -> x6, starting transfers between devices: 3.86 us -> 8.13 us  [the longest x3 5.51 us: local(): lax.ppermute(part, 'seq', [(i, (i + k) % seq_count) for i in range(seq_co...]
    pallas_call x13 -> x14, Pallas kernels: 20.5 us -> 21.9 us  [call(): pl.pallas_call(body, out_shape=list(outs), grid_spec=spec, compiler_param...]
    ppermute x3 -> x6, waiting for transfers between devices: 14.8 us -> 15.1 us  [the longest x3 9.05 us: pass_back(): lax.ppermute(value, 'seq', [(seq_count - stage, seq_count - 1 - stage)])]
  transfers between devices with their start and end apart: 14 -> 15, of which waited for: 9 -> 8; matrix products, arithmetic and copies ran while one was open for 0% -> 0% of each run, Pallas kernels for 18% -> 22%
where the time goes in v1:
time: 88 us; the launch traced here: 87.8 us
  waiting for transfers between devices  39.9 us (45%)
  starting transfers between devices  24.3 us (28%)
  Pallas kernels  21.9 us (25%)
    ppermute x6, waiting for transfers between devices, swap(): lax.ppermute(value, axis, [(i, i ^ bit) for i in range(lax.axis_size(axis...  22.1 us
    pallas_call x14, Pallas kernels, call(): pl.pallas_call(body, out_shape=list(outs), grid_spec=spec, compiler_param...  21.9 us
    ppermute x3, starting transfers between devices, shift_up(): lax.ppermute(value, 'seq', [(i, i + k) for i in range(count - k)])  9.28 us
    ppermute x3, waiting for transfers between devices, pass_back(): lax.ppermute(value, 'seq', [(seq_count - stage, seq_count - 1 - stage)])  9.05 us
    ppermute x6, starting transfers between devices, swap(): lax.ppermute(value, axis, [(i, i ^ bit) for i in range(lax.axis_size(axis...  6.85 us
    ppermute x3, waiting for transfers between devices, local(): lax.ppermute(part, 'seq', [(i, (i + k) % seq_count) for i in range(seq_co...  6.1 us
    ppermute x3, starting transfers between devices, local(): lax.ppermute(part, 'seq', [(i, (i + k) % seq_count) for i in range(seq_co...  5.51 us
    ppermute x3, waiting for transfers between devices, shift_up(): lax.ppermute(value, 'seq', [(i, i + k) for i in range(count - k)])  2.68 us
  transfers between devices with their start and end apart: 15, of which 8 were waited for; matrix products, arithmetic and copies ran while one was open for 0% of the time, Pallas kernels for 22%

profile of v1, /device:TPU:0, one launch (start us, length us, event | category | flops | bytes accessed | tf_op | source)
XLA Modules:
  0.0 87.8 jit_solution(11315038638000373238)
XLA Ops:
  0.6 3.1 %collective-permute-start = (bf16[512,1536]{1,0:T(8,128)(2,1)}, bf16[512,1536]{1,0:T(8,128)(2,1)S(1)}, u32[]{:S(2)}, u32[]{:S(2)}) collective-permute-start(bf16[512,1536]{1,0:T(8,128)(2,1)} %bitcast.12), channel_id=1, source_target_pairs={{0,1},{1,0},{2,3},{3,2},{4,5},{5,4},{6,7},{7,6},{8,9},{9,8},{10,11... | collective-permute-start | bytes 4718600 | tf_op jit(solution)/shard_map/ppermute | solution.py:313
  3.8 3.1 %shard_map.93 = (bf16[4,128,128]{2,1,0:T(8,128)(2,1)S(1)}, f32[8,512]{1,0:T(8,128)S(1)}, f32[512,8]{1,0:T(8,128)S(1)}, f32[4,2048]{1,0:T(4,128)S(1)}, bf16[512,5...) custom-call(s32[4]{0:T(128)S(1)} %pad_add_fusion.place, f32[4,2048]{1,0:T(4,128)} %bitcast.18, ...), custom_call_target="tpu_custom_call" | custom-call | tf_op jit(solution)/shard_map/pallas_call | solution.py:43
  6.9 5.5 %collective-permute-start.3 = (bf16[4,128,128]{2,1,0:T(8,128)(2,1)S(1)}, bf16[4,128,128]{2,1,0:T(8,128)(2,1)S(1)}, u32[]{:S(2)}, u32[]{:S(2)}) collective-permute-start(bf16[4,128,128]{2,1,0:T(8,128)(2,1)S(1)} %get-tuple-element.52), channel_id=1, source_target_pairs={{0,6},{1,7},{8,14},{9,15},{16,22},{17,23},{24,30},{25,31}} | collective-permute-start | bytes 393224 | tf_op jit(solution)/shard_map/ppermute | solution.py:305
  12.4 1.3 %collective-permute-start.2 = (bf16[4,128,128]{2,1,0:T(8,128)(2,1)S(1)}, bf16[4,128,128]{2,1,0:T(8,128)(2,1)S(1)}, u32[]{:S(2)}, u32[]{:S(2)}) collective-permute-start(bf16[4,128,128]{2,1,0:T(8,128)(2,1)S(1)} %get-tuple-element.52), channel_id=1, source_target_pairs={{0,4},{2,6},{1,5},{3,7},{8,12},{10,14},{9,13},{11,15},{16,20},{18,... | collective-permute-start | bytes 393224 | tf_op jit(solution)/shard_map/ppermute | solution.py:305
  13.7 2.5 %collective-permute-start.1 = (bf16[4,128,128]{2,1,0:T(8,128)(2,1)S(1)}, bf16[4,128,128]{2,1,0:T(8,128)(2,1)S(1)}, u32[]{:S(2)}, u32[]{:S(2)}) collective-permute-start(bf16[4,128,128]{2,1,0:T(8,128)(2,1)S(1)} %get-tuple-element.52), channel_id=1, source_target_pairs={{0,2},{2,4},{4,6},{1,3},{3,5},{5,7},{8,10},{10,12},{12,14},{9,11},... | collective-permute-start | bytes 393224 | tf_op jit(solution)/shard_map/ppermute | solution.py:305
  16.2 1.6 %shard_map.94 = (bf16[4,3,256,256]{3,2,1,0:T(8,128)(2,1)S(1)}, f32[512,512]{1,0:T(8,128)S(1)}) custom-call(bf16[512,512]{1,0:T(8,128)(2,1)S(1)} %get-tuple-element.60.query_ref, bf16[512,512]{1,0:T(8,128)(2,1)S(1)} %get-tuple-element.46.key_ref, bf16[512,512]{1,0:T(8,128)(2,1)S(1)} %get-tuple-element.47.value_ref, f32[8,512]{1,0:T(8,128)S(1)} %get-tuple-element.49.row_ref, ...), custom_call_target="tpu_custom_call" | custom-call | tf_op jit(solution)/shard_map/pallas_call | solution.py:43
  17.8 1.3 %collective-permute-done.2.refs_1_ = bf16[4,128,128]{2,1,0:T(8,128)(2,1)S(1)} collective-permute-done((bf16[4,128,128]{2,1,0:T(8,128)(2,1)S(1)}, bf16[4,128,128]{2,1,0:T(8,128)(2,1)S(1)}, u32[]{:S(2)}, u32[]{:S(2)}) %collective-permute-start.2) | collective-permute-done | bytes 131104 | tf_op jit(solution)/shard_map/ppermute | solution.py:305
  19.1 1.4 %collective-permute-done.1.refs_0_ = bf16[4,128,128]{2,1,0:T(8,128)(2,1)S(1)} collective-permute-done((bf16[4,128,128]{2,1,0:T(8,128)(2,1)S(1)}, bf16[4,128,128]{2,1,0:T(8,128)(2,1)S(1)}, u32[]{:S(2)}, u32[]{:S(2)}) %collective-permute-start.1) | collective-permute-done | bytes 131104 | tf_op jit(solution)/shard_map/ppermute | solution.py:305
  20.5 2.1 %shard_map.95 = (bf16[512,512]{1,0:T(8,128)(2,1)S(1)}, bf16[4,128,128]{2,1,0:T(8,128)(2,1)S(1)}, bf16[768,512]{1,0:T(8,128)(2,1)S(1)}, bf16[768,512]{1,0:T(8,128)(2,1)S(1)}) custom-call(s32[4]{0:T(128)S(1)} %pad_add_fusion.place, f32[4,2048]{1,0:T(4,128)S(1)} %get-tuple-element.48.decay_ref, bf16[512,512]{1,0:T(8,128)(2,1)S(1)} %get-tuple-element.60.query_ref, ...), custom_call_target="tpu_custom_call" | custom-call | tf_op jit(solution)/shard_map/pallas_call | solution.py:43
  22.7 2.3 %collective-permute-done.4.other_ref = bf16[768,512]{1,0:T(8,128)(2,1)S(1)} collective-permute-done((bf16[768,512]{1,0:T(8,128)(2,1)S(1)}, bf16[768,512]{1,0:T(8,128)(2,1)S(1)}, u32[]{:S(2)}, u32[]{:S(2)}) %collective-permute-start.4) | collective-permute-done | bytes 786464 | tf_op jit(solution)/shard_map/ppermute | solution.py:313
  25.7 1.6 %shard_map.97.refs_0_ = f32[512,512]{1,0:T(8,128)S(1)} custom-call(s32[4]{0:T(128)S(1)} %pad_add_fusion.place, bf16[512,1536]{1,0:T(8,128)(2,1)S(1)} %bitcast.14, bf16[512,3072]{1,0:T(8,128)(2,1)S(1)} %copy-done), custom_call_target="tpu_custom_call" | custom-call | tf_op jit(solution)/shard_map/pallas_call | solution.py:43
  27.2 11.0 %collective-permute-done.grad_ref = bf16[512,1536]{1,0:T(8,128)(2,1)S(1)} collective-permute-done((bf16[512,1536]{1,0:T(8,128)(2,1)}, bf16[512,1536]{1,0:T(8,128)(2,1)S(1)}, u32[]{:S(2)}, u32[]{:S(2)}) %collective-permute-start) | collective-permute-done | bytes 1572896 | tf_op jit(solution)/shard_map/ppermute | solution.py:313
  38.3 1.6 %shard_map.98 = (bf16[768,512]{1,0:T(8,128)(2,1)S(1)}, bf16[768,512]{1,0:T(8,128)(2,1)S(1)}) custom-call(s32[4]{0:T(128)S(1)} %pad_add_fusion.place, bf16[512,1536]{1,0:T(8,128)(2,1)S(1)} %collective-permute-done.grad_ref, bf16[512,512]{1,0:T(8,128)(2,1)S(1)} %get-tuple-element.58.attn_ref), custom_call_target="tpu_custom_call" | custom-call | tf_op jit(solution)/shard_map/pallas_call | solution.py:43
  39.9 1.9 %shard_map.99 = (bf16[512,512]{1,0:T(8,128)(2,1)S(1)}, bf16[4,128,128]{2,1,0:T(8,128)(2,1)S(1)}) custom-call(s32[4]{0:T(128)S(1)} %pad_add_fusion.place, bf16[512,1536]{1,0:T(8,128)(2,1)S(1)} %collective-permute-done.grad_ref, bf16[512,3072]{1,0:T(8,128)(2,1)S(1)} %copy-done, bf16[512,512]{1,0:T(8,128)(2,1)S(1)} %get-tuple-element.60.query_ref, ...), custom_call_target="tpu_custom_call" | custom-call | tf_op jit(solution)/shard_map/pallas_call | solution.py:43
  42.9 1.9 %collective-permute-start.9 = (bf16[2,192,512]{2,1,0:T(8,128)(2,1)S(1)}, bf16[2,192,512]{2,1,0:T(8,128)(2,1)S(1)}, u32[]{:S(2)}, u32[]{:S(2)}) collective-permute-start(bf16[2,192,512]{2,1,0:T(8,128)(2,1)S(1)} %get-tuple-element.75), channel_id=1, source_target_pairs={{0,2},{2,0},{4,6},{6,4},{1,3},{3,1},{5,7},{7,5},{8,10},{10,8},{12,... | collective-permute-start | bytes 1179656 | tf_op jit(solution)/shard_map/ppermute | solution.py:313
  45.0 2.8 %collective-permute-start.7 = (bf16[192,512]{1,0:T(8,128)(2,1)S(1)}, bf16[192,512]{1,0:T(8,128)(2,1)S(1)}, u32[]{:S(2)}, u32[]{:S(2)}) collective-permute-start(bf16[192,512]{1,0:T(8,128)(2,1)S(1)} %get-tuple-element.72), channel_id=1, source_target_pairs={{0,4},{2,6},{4,0},{6,2},{1,5},{3,7},{5,1},{7,3},{8,12},{10,14},{12... | collective-permute-start | bytes 589832 | tf_op jit(solution)/shard_map/ppermute | solution.py:392
  47.8 2.5 %collective-permute-start.8 = (bf16[192,512]{1,0:T(8,128)(2,1)S(1)}, bf16[192,512]{1,0:T(8,128)(2,1)S(1)}, u32[]{:S(2)}, u32[]{:S(2)}) collective-permute-start(bf16[192,512]{1,0:T(8,128)(2,1)S(1)} %get-tuple-element.73), channel_id=1, source_target_pairs={{0,6},{2,0},{4,2},{6,4},{1,7},{3,1},{5,3},{7,5},{8,14},{10,8},{12,... | collective-permute-start | bytes 589832 | tf_op jit(solution)/shard_map/ppermute | solution.py:392
  51.0 4.1 %shard_map.101 = (bf16[512,512]{1,0:T(8,128)(2,1)}, f32[512,512]{1,0:T(8,128)S(1)}, f32[512,512]{1,0:T(8,128)S(1)}) custom-call(bf16[512,512]{1,0:T(8,128)(2,1)S(1)} %get-tuple-element.60.query_ref, bf16[512,512]{1,0:T(8,128)(2,1)S(1)} %get-tuple-element.46.key_ref, bf16[512,512]{1,0:T(8,128)(2,1)S(1)} %get-tuple-element.47.value_ref, ...), custom_call_target="tpu_custom_call" | custom-call | tf_op jit(solution)/shard_map/pallas_call | solution.py:43
  55.0 8.4 %collective-permute-done.9.other_ref = bf16[2,192,512]{2,1,0:T(8,128)(2,1)S(1)} collective-permute-done((bf16[2,192,512]{2,1,0:T(8,128)(2,1)S(1)}, bf16[2,192,512]{2,1,0:T(8,128)(2,1)S(1)}, u32[]{:S(2)}, u32[]{:S(2)}) %collective-permute-start.9) | collective-permute-done | bytes 393248 | tf_op jit(solution)/shard_map/ppermute | solution.py:313
  65.0 6.1 %collective-permute-done.8.refs_3_ = bf16[192,512]{1,0:T(8,128)(2,1)S(1)} collective-permute-done((bf16[192,512]{1,0:T(8,128)(2,1)S(1)}, bf16[192,512]{1,0:T(8,128)(2,1)S(1)}, u32[]{:S(2)}, u32[]{:S(2)}) %collective-permute-start.8) | collective-permute-done | bytes 196640 | tf_op jit(solution)/shard_map/ppermute | solution.py:392
  71.8 1.7 %collective-permute-start.14 = (bf16[192,512]{1,0:T(8,128)(2,1)S(1)}, bf16[192,512]{1,0:T(8,128)(2,1)S(1)}, u32[]{:S(2)}, u32[]{:S(2)}) collective-permute-start(bf16[192,512]{1,0:T(8,128)(2,1)S(1)} %get-tuple-element.85), channel_id=1, source_target_pairs={{0,16},{8,24},{16,0},{24,8},{1,17},{9,25},{17,1},{25,9},{2,18},{10... | collective-permute-start | bytes 589832 | tf_op jit(solution)/shard_map/ppermute | solution.py:313
  74.2 1.3 %collective-permute-start.13 = (bf16[4,128,128]{2,1,0:T(8,128)(2,1)S(1)}, bf16[4,128,128]{2,1,0:T(8,128)(2,1)S(1)}, u32[]{:S(2)}, u32[]{:S(2)}) collective-permute-start(bf16[4,128,128]{2,1,0:T(8,128)(2,1)S(1)} %shard_map.105), channel_id=1, source_target_pairs={{2,0},{3,1},{10,8},{11,9},{18,16},{19,17},{26,24},{27,25}} | collective-permute-start | bytes 393224 | tf_op jit(solution)/shard_map/ppermute | solution.py:421
  75.5 9.0 %collective-permute-done.13.refs_2_ = bf16[4,128,128]{2,1,0:T(8,128)(2,1)S(1)} collective-permute-done((bf16[4,128,128]{2,1,0:T(8,128)(2,1)S(1)}, bf16[4,128,128]{2,1,0:T(8,128)(2,1)S(1)}, u32[]{:S(2)}, u32[]{:S(2)}) %collective-permute-start.13) | collective-permute-done | bytes 131104 | tf_op jit(solution)/shard_map/ppermute | solution.py:421
  84.5 2.4 %shard_map.106 = (bf16[512,512]{1,0:T(8,128)(2,1)}, bf16[512,512]{1,0:T(8,128)(2,1)}) custom-call(s32[4]{0:T(128)S(1)} %pad_add_fusion.place, f32[4,2048]{1,0:T(4,128)S(1)} %get-tuple-element.48.decay_ref, bf16[512,512]{1,0:T(8,128)(2,1)S(1)} %get-tuple-element.46.key_ref, bf16[512,512]{1,0:T(8,128)(2,1)S(1)} %get-tuple-element.47.value_ref, ...), custom_call_target="tpu_custom_call" | custom-call | tf_op jit(solution)/shard_map/pallas_call | solution.py:43
  (26 shorter events, 6.7 us)
Async XLA Ops:
  0.6 37.7 %collective-permute-start = (bf16[512,1536]{1,0:T(8,128)(2,1)}, bf16[512,1536]{1,0:T(8,128)(2,1)S(1)}, u32[]{:S(2)}, u32[]{:S(2)}) collective-permute-start(bf16[512,1536]{1,0:T(8,128)(2,1)} %bitcast.12), channel_id=1, source_target_pairs={{0,1},{1,0},{2,3},{3,2},{4,5},{5,4},{6,7},{7,6},{8,9},{9,8},{10,11... | collective-permute-start | bytes 4718600 | tf_op jit(solution)/shard_map/ppermute | solution.py:313
  3.8 16.8 %copy-start.1 = (bf16[1,512,1536]{2,1,0:T(8,128)(2,1)S(1)}, bf16[1,512,1536]{2,1,0:T(8,128)(2,1)}, u32[]{:S(2)}) copy-start(bf16[1,512,1536]{2,1,0:T(8,128)(2,1)} %param.11) | copy-start | bytes 4718596
  6.9 10.9 %collective-permute-start.3 = (bf16[4,128,128]{2,1,0:T(8,128)(2,1)S(1)}, bf16[4,128,128]{2,1,0:T(8,128)(2,1)S(1)}, u32[]{:S(2)}, u32[]{:S(2)}) collective-permute-start(bf16[4,128,128]{2,1,0:T(8,128)(2,1)S(1)} %get-tuple-element.52), channel_id=1, source_target_pairs={{0,6},{1,7},{8,14},{9,15},{16,22},{17,23},{24,30},{25,31}} | collective-permute-start | bytes 393224 | tf_op jit(solution)/shard_map/ppermute | solution.py:305
  12.4 6.7 %collective-permute-start.2 = (bf16[4,128,128]{2,1,0:T(8,128)(2,1)S(1)}, bf16[4,128,128]{2,1,0:T(8,128)(2,1)S(1)}, u32[]{:S(2)}, u32[]{:S(2)}) collective-permute-start(bf16[4,128,128]{2,1,0:T(8,128)(2,1)S(1)} %get-tuple-element.52), channel_id=1, source_target_pairs={{0,4},{2,6},{1,5},{3,7},{8,12},{10,14},{9,13},{11,15},{16,20},{18,... | collective-permute-start | bytes 393224 | tf_op jit(solution)/shard_map/ppermute | solution.py:305
  13.7 6.8 %collective-permute-start.1 = (bf16[4,128,128]{2,1,0:T(8,128)(2,1)S(1)}, bf16[4,128,128]{2,1,0:T(8,128)(2,1)S(1)}, u32[]{:S(2)}, u32[]{:S(2)}) collective-permute-start(bf16[4,128,128]{2,1,0:T(8,128)(2,1)S(1)} %get-tuple-element.52), channel_id=1, source_target_pairs={{0,2},{2,4},{4,6},{1,3},{3,5},{5,7},{8,10},{10,12},{12,14},{9,11},... | collective-permute-start | bytes 393224 | tf_op jit(solution)/shard_map/ppermute | solution.py:305
  20.5 5.1 %copy-start = (bf16[512,3072]{1,0:T(8,128)(2,1)S(1)}, bf16[512,3072]{1,0:T(8,128)(2,1)}, u32[]{:S(2)}) copy-start(bf16[512,3072]{1,0:T(8,128)(2,1)} %out_ref.2) | copy-start | bytes 9437188
  22.6 2.4 %collective-permute-start.4 = (bf16[768,512]{1,0:T(8,128)(2,1)S(1)}, bf16[768,512]{1,0:T(8,128)(2,1)S(1)}, u32[]{:S(2)}, u32[]{:S(2)}) collective-permute-start(bf16[768,512]{1,0:T(8,128)(2,1)S(1)} %get-tuple-element.55), channel_id=1, source_target_pairs={{0,8},{8,0},{16,24},{24,16},{1,9},{9,1},{17,25},{25,17},{2,10},{10... | collective-permute-start | bytes 2359304 | tf_op jit(solution)/shard_map/ppermute | solution.py:313
  39.9 2.4 %collective-permute-start.5 = (bf16[768,512]{1,0:T(8,128)(2,1)S(1)}, bf16[768,512]{1,0:T(8,128)(2,1)S(1)}, u32[]{:S(2)}, u32[]{:S(2)}) collective-permute-start(bf16[768,512]{1,0:T(8,128)(2,1)S(1)} %get-tuple-element.64), channel_id=1, source_target_pairs={{0,8},{8,0},{16,24},{24,16},{1,9},{9,1},{17,25},{25,17},{2,10},{10... | collective-permute-start | bytes 2359304 | tf_op jit(solution)/shard_map/ppermute | solution.py:313
  42.9 20.5 %collective-permute-start.9 = (bf16[2,192,512]{2,1,0:T(8,128)(2,1)S(1)}, bf16[2,192,512]{2,1,0:T(8,128)(2,1)S(1)}, u32[]{:S(2)}, u32[]{:S(2)}) collective-permute-start(bf16[2,192,512]{2,1,0:T(8,128)(2,1)S(1)} %get-tuple-element.75), channel_id=1, source_target_pairs={{0,2},{2,0},{4,6},{6,4},{1,3},{3,1},{5,7},{7,5},{8,10},{10,8},{12,... | collective-permute-start | bytes 1179656 | tf_op jit(solution)/shard_map/ppermute | solution.py:313
  44.8 20.2 %collective-permute-start.6 = (bf16[192,512]{1,0:T(8,128)(2,1)S(1)}, bf16[192,512]{1,0:T(8,128)(2,1)S(1)}, u32[]{:S(2)}, u32[]{:S(2)}) collective-permute-start(bf16[192,512]{1,0:T(8,128)(2,1)S(1)} %get-tuple-element.71), channel_id=1, source_target_pairs={{0,2},{2,4},{4,6},{6,0},{1,3},{3,5},{5,7},{7,1},{8,10},{10,12},{12... | collective-permute-start | bytes 589832 | tf_op jit(solution)/shard_map/ppermute | solution.py:392
  45.0 19.9 %collective-permute-start.7 = (bf16[192,512]{1,0:T(8,128)(2,1)S(1)}, bf16[192,512]{1,0:T(8,128)(2,1)S(1)}, u32[]{:S(2)}, u32[]{:S(2)}) collective-permute-start(bf16[192,512]{1,0:T(8,128)(2,1)S(1)} %get-tuple-element.72), channel_id=1, source_target_pairs={{0,4},{2,6},{4,0},{6,2},{1,5},{3,7},{5,1},{7,3},{8,12},{10,14},{12... | collective-permute-start | bytes 589832 | tf_op jit(solution)/shard_map/ppermute | solution.py:392
  47.8 23.2 %collective-permute-start.8 = (bf16[192,512]{1,0:T(8,128)(2,1)S(1)}, bf16[192,512]{1,0:T(8,128)(2,1)S(1)}, u32[]{:S(2)}, u32[]{:S(2)}) collective-permute-start(bf16[192,512]{1,0:T(8,128)(2,1)S(1)} %get-tuple-element.73), channel_id=1, source_target_pairs={{0,6},{2,0},{4,2},{6,4},{1,7},{3,1},{5,3},{7,5},{8,14},{10,8},{12,... | collective-permute-start | bytes 589832 | tf_op jit(solution)/shard_map/ppermute | solution.py:392
  50.3 13.3 %collective-permute-start.11 = (bf16[4,128,128]{2,1,0:T(8,128)(2,1)S(1)}, bf16[4,128,128]{2,1,0:T(8,128)(2,1)S(1)}, u32[]{:S(2)}, u32[]{:S(2)}) collective-permute-start(bf16[4,128,128]{2,1,0:T(8,128)(2,1)S(1)} %get-tuple-element.82.back_ref), channel_id=1, source_target_pairs={{6,4},{7,5},{14,12},{15,13},{22,20},{23,21},{30,28},{31,29}} | collective-permute-start | bytes 393224 | tf_op jit(solution)/shard_map/ppermute | solution.py:421
  63.5 7.6 %collective-permute-start.10 = (bf16[192,512]{1,0:T(8,128)(2,1)S(1)}, bf16[192,512]{1,0:T(8,128)(2,1)S(1)}, u32[]{:S(2)}, u32[]{:S(2)}) collective-permute-start(bf16[192,512]{1,0:T(8,128)(2,1)S(1)} %get-tuple-element.77), channel_id=1, source_target_pairs={{0,4},{2,6},{4,0},{6,2},{1,5},{3,7},{5,1},{7,3},{8,12},{10,14},{12... | collective-permute-start | bytes 589832 | tf_op jit(solution)/shard_map/ppermute | solution.py:313
  64.3 9.2 %collective-permute-start.12 = (bf16[4,128,128]{2,1,0:T(8,128)(2,1)S(1)}, bf16[4,128,128]{2,1,0:T(8,128)(2,1)S(1)}, u32[]{:S(2)}, u32[]{:S(2)}) collective-permute-start(bf16[4,128,128]{2,1,0:T(8,128)(2,1)S(1)} %shard_map.104), channel_id=1, source_target_pairs={{4,2},{5,3},{12,10},{13,11},{20,18},{21,19},{28,26},{29,27}} | collective-permute-start | bytes 393224 | tf_op jit(solution)/shard_map/ppermute | solution.py:421
  71.8 15.2 %collective-permute-start.14 = (bf16[192,512]{1,0:T(8,128)(2,1)S(1)}, bf16[192,512]{1,0:T(8,128)(2,1)S(1)}, u32[]{:S(2)}, u32[]{:S(2)}) collective-permute-start(bf16[192,512]{1,0:T(8,128)(2,1)S(1)} %get-tuple-element.85), channel_id=1, source_target_pairs={{0,16},{8,24},{16,0},{24,8},{1,17},{9,25},{17,1},{25,9},{2,18},{10... | collective-permute-start | bytes 589832 | tf_op jit(solution)/shard_map/ppermute | solution.py:313
  74.2 10.3 %collective-permute-start.13 = (bf16[4,128,128]{2,1,0:T(8,128)(2,1)S(1)}, bf16[4,128,128]{2,1,0:T(8,128)(2,1)S(1)}, u32[]{:S(2)}, u32[]{:S(2)}) collective-permute-start(bf16[4,128,128]{2,1,0:T(8,128)(2,1)S(1)} %shard_map.105), channel_id=1, source_target_pairs={{2,0},{3,1},{10,8},{11,9},{18,16},{19,17},{26,24},{27,25}} | collective-permute-start | bytes 393224 | tf_op jit(solution)/shard_map/ppermute | solution.py:421

commit v2 on v1

--- a/solution.py
+++ b/solution.py
@@ -12,6 +12,7 @@
 F32 = jnp.float32
 BF16 = jnp.bfloat16
 TILE = 256
+FIRST = 256
 GRANT = 24 * 1024 * 1024
 
 
@@ -158,11 +159,12 @@
         attn_ref[:, at] = (within_ref[:, at] + dot_nn(scaled.astype(BF16), carried)).astype(BF16)
 
 
-def project(place, grad_ref, attn_ref, send_ref, keep_ref, scale):
-    half = keep_ref.shape[0]
+def project(place, grad_ref, attn_ref, send_ref, keep_ref, scale, start=0):
+    half, wide = keep_ref.shape
+    attn = attn_ref[:, start : start + wide]
     for core, into in ((1 - place[1], send_ref), (place[1], keep_ref)):
         at = pl.ds(pl.multiple_of(core * half, 128), half)
-        into[...] = (dot_tn(grad_ref[:, at], attn_ref[...]) * scale).astype(BF16)
+        into[...] = (dot_tn(grad_ref[:, at], attn) * scale).astype(BF16)
 
 
 def attention_kernel(place, decay_ref, query_ref, within_ref, column_ref, *refs, heads):
@@ -176,8 +178,8 @@
     project(place, grad_ref, attn_ref, send_ref, keep_ref, scale)
 
 
-def projection_kernel(place, grad_ref, attn_ref, send_ref, keep_ref, *, scale):
-    project(place, grad_ref, attn_ref, send_ref, keep_ref, scale)
+def projection_kernel(place, grad_ref, attn_ref, send_ref, keep_ref, *, scale, start):
+    project(place, grad_ref, attn_ref, send_ref, keep_ref, scale, start)
 
 
 def half_columns(out_ref, index, count):
@@ -262,11 +264,20 @@
         dv_ref[:, at] = (inner_v_ref[:, at] + dot_nn(keys, back)).astype(BF16)
 
 
+def owner_turns(bit):
+    return (3 - bit, 0, 3, bit)
+
+
+def sum_kernel(mine_ref, other_ref, keep_ref, send_ref):
+    total = mine_ref[...].astype(F32) + other_ref[...].astype(F32)
+    keep_ref[...] = total
+    send_ref[...] = total.astype(BF16)
+
+
 def pieces_kernel(place, mine_ref, other_ref, keep_ref, send_ref):
     rows = keep_ref.shape[1]
-    for n in range(4):
-        owner = place[0] ^ (2, 0, 3, 1)[n]
-        at = pl.ds(pl.multiple_of(owner * rows, 16), rows)
+    for n, turn in enumerate(owner_turns(1)):
+        at = pl.ds(pl.multiple_of((place[0] ^ turn) * rows, 16), rows)
         total = mine_ref[at, :].astype(F32) + other_ref[at, :].astype(F32)
         if n < 2:
             keep_ref[n] = total
@@ -274,15 +285,31 @@
             send_ref[n - 2] = total.astype(BF16)
 
 
-def direct_kernel(place, mine_ref, other_ref, keep_ref, *send_refs):
-    count, rows = len(send_refs) + 1, keep_ref.shape[0]
-    for k in range(count):
-        at = pl.ds(pl.multiple_of(lax.rem(place[0] + k, count) * rows, 16), rows)
-        total = mine_ref[at, :].astype(F32) + other_ref[at, :].astype(F32)
-        if k == 0:
-            keep_ref[...] = total
+def own_kernel(place, mine_ref, other_ref, keep_ref, send_ref, later_keep_ref, later_send_ref):
+    _, rows, wide = keep_ref.shape
+    for n, turn in enumerate(owner_turns(1)):
+        at = pl.ds(pl.multiple_of((place[0] ^ turn) * rows, 16), rows)
+        total = mine_ref[at, :wide].astype(F32) + other_ref[at, :wide].astype(F32)
+        if n < 2:
+            keep_ref[n] = total
         else:
-            send_refs[k - 1][...] = total.astype(BF16)
+            send_ref[n - 2] = total.astype(BF16)
+    later = mine_ref[:, wide:].astype(F32) + other_ref[:, wide:].astype(F32)
+    later_keep_ref[...] = later
+    later_send_ref[...] = later.astype(BF16)
+
+
+def later_kernel(place, own_ref, own_other_ref, far_ref, far_other_ref, keep_ref, send_ref):
+    rows = keep_ref.shape[1]
+    mine = place[2] == place[3]
+    for n, turn in enumerate(owner_turns(1)):
+        at = pl.ds(pl.multiple_of((place[0] ^ turn) * rows, 16), rows)
+        kept = jnp.where(mine, own_ref[at, :], far_ref[at, :])
+        came = jnp.where(mine, own_other_ref[at, :].astype(F32), far_other_ref[at, :].astype(F32))
+        if n < 2:
+            keep_ref[n] = kept + came
+        else:
+            send_ref[n - 2] = (kept + came).astype(BF16)
 
 
 def halve_kernel(mine_ref, other_ref, keep_ref, send_ref):
@@ -290,23 +317,37 @@
     keep_ref[...] = mine_ref[1] + other_ref[1].astype(F32)
 
 
-def finish_kernel(place, *refs):
-    own_ref, *own_others, far_ref, far_other_ref, keep_ref, send_ref = refs
-    own = own_ref[...]
-    for ref in own_others:
-        own = own + ref[...].astype(F32)
+def finish_kernel(place, own_ref, own_other_ref, far_ref, far_other_ref, keep_ref, send_ref):
+    own = own_ref[...] + own_other_ref[...].astype(F32)
     far = far_ref[...] + far_other_ref[...].astype(F32)
     mine = place[2] == place[3]
     send_ref[...] = jnp.where(mine, far, own).astype(BF16)
     keep_ref[...] = jnp.where(mine, own, far)
 
 
+def result_kernel(first_ref, crossed_ref, later_ref, later_other_ref, out_ref):
+    wide = first_ref.shape[1]
+    out_ref[:, :wide] = first_ref[...] + crossed_ref[...].astype(F32)
+    out_ref[:, wide:] = later_ref[...] + later_other_ref[...].astype(F32)
+
+
 def shift_up(value, count):
     return [lax.ppermute(value, "seq", [(i, i + k) for i in range(count - k)]) for k in range(1, count)]
 
 
 def shift_down(value, count):
     return [lax.ppermute(value, "seq", [(i, i - k) for i in range(k, count)]) for k in range(1, count)]
+
+
+def to_chip(value, own):
+    tensor_count = lax.axis_size("tensor")
+    pairs = []
+    for t in range(tensor_count):
+        target = t if own else 1 - t
+        for core in range(2):
+            start = (2 * (1 - target) + core) * tensor_count + t
+            pairs.append((start, (2 * target + core) * tensor_count + t))
+    return lax.ppermute(value, ("dp", "tensor"), pairs)
 
 
 def swap(value, axis, bit):
@@ -361,19 +402,11 @@
 
         quarter = (piece, features)
 
-        def spread(send, keep, *behind):
-            came = swap(send, "dp", 1)
-            stay, go = call(
-                pieces_kernel,
-                [shape((2, *quarter), F32), shape((2, *quarter), BF16)],
-                [after(keep, *behind), came],
-                place,
-            )
-            return stay, swap(go, "seq", 1)
+        first_part, later_part = (piece, FIRST), (piece, features - FIRST)
 
         def halve(stay, came, *behind):
-            stay, go = call(halve_kernel, [shape(quarter, F32), shape(quarter, BF16)], [after(stay, *behind), came])
-            return stay, swap(go, "seq", 2)
+            dims = stay.shape[1:]
+            return call(halve_kernel, [shape(dims, F32), shape(dims, BF16)], [after(stay, *behind), came])
 
         attn, carried, send, keep = call(
             functools.partial(attention_project_kernel, heads=heads, scale=scale),
@@ -381,21 +414,48 @@
             [*attend_args, grad, *received],
             place,
         )
-        came = swap(send, "dp", 1)
-        own_stay, *own_parts = call(
-            direct_kernel,
-            [shape(quarter, F32)] + [shape(quarter, BF16)] * (seq_count - 1),
-            [keep, came],
+        own_swap = swap(send, "dp", 1)
+        own_stay, go, own_later, later_go = call(
+            own_kernel,
+            [
+                shape((2, *first_part), F32),
+                shape((2, *first_part), BF16),
+                shape((dest, features - FIRST), F32),
+                shape((dest, features - FIRST), BF16),
+            ],
+            [keep, own_swap],
             place,
         )
-        own_came = [
-            lax.ppermute(part, "seq", [(i, (i + k) % seq_count) for i in range(seq_count)])
-            for k, part in enumerate(own_parts, 1)
-        ]
+        own_came = swap(go, "seq", 1)
+        own_later_came = to_chip(later_go, True)
         (half,) = call(grad_attn_half_kernel, [token_f32], [grad, after(w_out, own_stay)], place)
-        send, keep_far = call(
-            functools.partial(projection_kernel, scale=scale), parts, [other, after(attn, half)], place
-        )
+
+        own_stay, go = halve(own_stay, own_came, half)
+        own_came = swap(go, "seq", 2)
+
+        def project_far(start, width, *behind):
+            send, keep = call(
+                functools.partial(projection_kernel, scale=scale, start=start),
+                [shape((dest, width), BF16)] * 2,
+                [other, after(attn, *behind)],
+                place,
+            )
+            return keep, swap(send, "dp", 1)
+
+        later_keep, later_swap = project_far(FIRST, features - FIRST, own_stay)
+        far_keep, far_swap = project_far(0, FIRST, later_keep)
+        later_shape = (dest, features - FIRST)
+        later_stay, go = call(
+            sum_kernel, [shape(later_shape, F32), shape(later_shape, BF16)], [after(later_keep, far_keep), later_swap]
+        )
+        later_came = to_chip(go, False)
+        far_stay, go = call(
+            pieces_kernel,
+            [shape((2, *first_part), F32), shape((2, *first_part), BF16)],
+            [after(far_keep, later_stay), far_swap],
+            place,
+        )
+        far_came = swap(go, "seq", 1)
         last = (half,)
     else:
         attn, carried = call(
@@ -409,7 +469,7 @@
         last, keep = (), attn
 
     if paired:
-        keep = keep_far
+        keep = far_stay
     grad_attn, back = call(
         functools.partial(grad_attn_kernel, heads=heads),
         [token_bf16, state_shape],
@@ -422,8 +482,7 @@
 
     returned = [pass_back(back, 1)] if paired else shift_down(back, seq_count)
     if paired:
-        far_stay, far_came = spread(send, keep_far, back)
-        grad_attn = after(grad_attn, far_stay)
+        grad_attn = after(grad_attn, back)
     grad_queries, inner_keys, inner_values = call(
         functools.partial(inner_kernel, heads=heads),
         [final((rows, features), BF16), token_f32, token_f32],
@@ -440,16 +499,26 @@
             return pass_back(passed, stage)
 
         returned.append(chain(2, inner_keys))
-        far_stay, far_came = halve(far_stay, far_came, inner_keys)
+        later_stay, go = call(
+            later_kernel,
+            [shape((2, *later_part), F32), shape((2, *later_part), BF16)],
+            [own_later, own_later_came, after(later_stay, inner_keys), later_came],
+            place,
+        )
+        later_came = swap(go, "seq", 1)
+        far_stay, go = halve(far_stay, far_came, later_stay)
+        far_came = swap(go, "seq", 2)
         returned.append(chain(3, far_stay))
-        keep, send = call(
+        later_stay, go = halve(later_stay, later_came, far_stay)
+        later_came = swap(go, "seq", 2)
+        first_keep, send = call(
             finish_kernel,
-            [shape(quarter, F32), shape(quarter, BF16)],
-            [own_stay, *own_came, far_stay, far_came],
+            [shape(first_part, F32), shape(first_part, BF16)],
+            [own_stay, own_came, after(far_stay, later_stay), far_came],
             place,
         )
         crossed = swap(send, "dp", 2)
-        inner_keys = after(inner_keys, keep)
+        inner_keys = after(inner_keys, first_keep)
     grad_keys, grad_values = call(
         functools.partial(outer_kernel, heads=heads, chained=paired),
         [final((rows, features), BF16)] * 2,
@@ -457,7 +526,11 @@
         place,
     )
     if paired:
-        grad_w = keep + crossed.astype(F32)
+        (grad_w,) = call(
+            result_kernel,
+            [final(quarter, F32)],
+            [after(first_keep, grad_keys), crossed, later_stay, later_came],
+        )
     return grad_queries[None], grad_keys[None], grad_values[None], grad_w
 
 

time: 88 us -> 83.2 us (0.945)
  waiting for transfers between devices: 39.9 us -> 23.2 us
  starting transfers between devices: 24.3 us -> 34.7 us
  Pallas kernels: 21.9 us -> 24.1 us
    ppermute x6 -> x11, starting transfers between devices: 6.85 us -> 16.8 us  [swap(): lax.ppermute(value, axis, [(i, i ^ bit) for i in range(lax.axis_size(axis...]
    ppermute x3, waiting for transfers between devices: 9.05 us -> 1.06 us  [pass_back(): lax.ppermute(value, 'seq', [(seq_count - stage, seq_count - 1 - stage)])]
    ppermute x3 -> x2, waiting for transfers between devices: 6.1 us -> 0.01 us  [to_chip(): return lax.ppermute(value, ('dp', 'tensor'), pairs)]
    ppermute x6 -> x11, waiting for transfers between devices: 22.1 us -> 19.5 us  [swap(): lax.ppermute(value, axis, [(i, i ^ bit) for i in range(lax.axis_size(axis...]
    pallas_call x14 -> x20, Pallas kernels: 21.9 us -> 24.1 us  [call(): pl.pallas_call(body, out_shape=list(outs), grid_spec=spec, compiler_param...]
    ppermute x3 -> x2, starting transfers between devices: 5.51 us -> 5.87 us  [to_chip(): return lax.ppermute(value, ('dp', 'tensor'), pairs)]
  transfers between devices with their start and end apart: 15 -> 19, of which waited for: 8 -> 9; matrix products, arithmetic and copies ran while one was open for 0% -> 0% of each run, Pallas kernels for 22% -> 27%
where the time goes in v2:
time: 83.2 us; the launch traced here: 82.9 us
  starting transfers between devices  34.7 us (42%)
  Pallas kernels  24.1 us (29%)
  waiting for transfers between devices  23.2 us (28%)
  between operations  0.86 us (1%)
    pallas_call x20, Pallas kernels, call(): pl.pallas_call(body, out_shape=list(outs), grid_spec=spec, compiler_param...  24.1 us
    ppermute x11, waiting for transfers between devices, swap(): lax.ppermute(value, axis, [(i, i ^ bit) for i in range(lax.axis_size(axis...  19.5 us
    ppermute x11, starting transfers between devices, swap(): lax.ppermute(value, axis, [(i, i ^ bit) for i in range(lax.axis_size(axis...  16.8 us
    ppermute x3, starting transfers between devices, shift_up(): lax.ppermute(value, 'seq', [(i, i + k) for i in range(count - k)])  9.28 us
    ppermute x2, starting transfers between devices, to_chip(): return lax.ppermute(value, ('dp', 'tensor'), pairs)  5.87 us
    ppermute x3, starting transfers between devices, pass_back(): lax.ppermute(value, 'seq', [(seq_count - stage, seq_count - 1 - stage)])  2.81 us
    ppermute x3, waiting for transfers between devices, shift_up(): lax.ppermute(value, 'seq', [(i, i + k) for i in range(count - k)])  2.67 us
  transfers between devices with their start and end apart: 19, of which 9 were waited for; matrix products, arithmetic and copies ran while one was open for 0% of the time, Pallas kernels for 27%

profile of v2, /device:TPU:0, one launch (start us, length us, event | category | flops | bytes accessed | tf_op | source)
XLA Modules:
  0.0 82.9 jit_solution(15709369874658093429)
XLA Ops:
  0.6 3.1 %collective-permute-start = (bf16[512,1536]{1,0:T(8,128)(2,1)}, bf16[512,1536]{1,0:T(8,128)(2,1)S(1)}, u32[]{:S(2)}, u32[]{:S(2)}) collective-permute-start(bf16[512,1536]{1,0:T(8,128)(2,1)} %bitcast.12), channel_id=1, source_target_pairs={{0,1},{1,0},{2,3},{3,2},{4,5},{5,4},{6,7},{7,6},{8,9},{9,8},{10,11... | collective-permute-start | bytes 4718600 | tf_op jit(solution)/shard_map/ppermute | solution.py:354
  3.8 3.1 %shard_map.93 = (bf16[4,128,128]{2,1,0:T(8,128)(2,1)S(1)}, f32[8,512]{1,0:T(8,128)S(1)}, f32[512,8]{1,0:T(8,128)S(1)}, f32[4,2048]{1,0:T(4,128)S(1)}, bf16[512,5...) custom-call(s32[4]{0:T(128)S(1)} %pad_add_fusion.place, f32[4,2048]{1,0:T(4,128)} %bitcast.18, ...), custom_call_target="tpu_custom_call" | custom-call | tf_op jit(solution)/shard_map/pallas_call | solution.py:44
  6.9 5.5 %collective-permute-start.3 = (bf16[4,128,128]{2,1,0:T(8,128)(2,1)S(1)}, bf16[4,128,128]{2,1,0:T(8,128)(2,1)S(1)}, u32[]{:S(2)}, u32[]{:S(2)}) collective-permute-start(bf16[4,128,128]{2,1,0:T(8,128)(2,1)S(1)} %get-tuple-element.69), channel_id=1, source_target_pairs={{0,6},{1,7},{8,14},{9,15},{16,22},{17,23},{24,30},{25,31}} | collective-permute-start | bytes 393224 | tf_op jit(solution)/shard_map/ppermute | solution.py:335
  12.4 1.3 %collective-permute-start.2 = (bf16[4,128,128]{2,1,0:T(8,128)(2,1)S(1)}, bf16[4,128,128]{2,1,0:T(8,128)(2,1)S(1)}, u32[]{:S(2)}, u32[]{:S(2)}) collective-permute-start(bf16[4,128,128]{2,1,0:T(8,128)(2,1)S(1)} %get-tuple-element.69), channel_id=1, source_target_pairs={{0,4},{2,6},{1,5},{3,7},{8,12},{10,14},{9,13},{11,15},{16,20},{18,... | collective-permute-start | bytes 393224 | tf_op jit(solution)/shard_map/ppermute | solution.py:335
  13.7 2.5 %collective-permute-start.1 = (bf16[4,128,128]{2,1,0:T(8,128)(2,1)S(1)}, bf16[4,128,128]{2,1,0:T(8,128)(2,1)S(1)}, u32[]{:S(2)}, u32[]{:S(2)}) collective-permute-start(bf16[4,128,128]{2,1,0:T(8,128)(2,1)S(1)} %get-tuple-element.69), channel_id=1, source_target_pairs={{0,2},{2,4},{4,6},{1,3},{3,5},{5,7},{8,10},{10,12},{12,14},{9,11},... | collective-permute-start | bytes 393224 | tf_op jit(solution)/shard_map/ppermute | solution.py:335
  16.2 1.6 %shard_map.94 = (bf16[4,3,256,256]{3,2,1,0:T(8,128)(2,1)S(1)}, f32[512,512]{1,0:T(8,128)S(1)}) custom-call(bf16[512,512]{1,0:T(8,128)(2,1)S(1)} %get-tuple-element.88.query_ref, bf16[512,512]{1,0:T(8,128)(2,1)S(1)} %get-tuple-element.63.key_ref, bf16[512,512]{1,0:T(8,128)(2,1)S(1)} %get-tuple-element.64.value_ref, f32[8,512]{1,0:T(8,128)S(1)} %get-tuple-element.66.row_ref, ...), custom_call_target="tpu_custom_call" | custom-call | tf_op jit(solution)/shard_map/pallas_call | solution.py:44
  19.1 1.4 %collective-permute-done.1.refs_0_ = bf16[4,128,128]{2,1,0:T(8,128)(2,1)S(1)} collective-permute-done((bf16[4,128,128]{2,1,0:T(8,128)(2,1)S(1)}, bf16[4,128,128]{2,1,0:T(8,128)(2,1)S(1)}, u32[]{:S(2)}, u32[]{:S(2)}) %collective-permute-start.1) | collective-permute-done | bytes 131104 | tf_op jit(solution)/shard_map/ppermute | solution.py:335
  20.5 2.1 %shard_map.95 = (bf16[512,512]{1,0:T(8,128)(2,1)S(1)}, bf16[4,128,128]{2,1,0:T(8,128)(2,1)S(1)}, bf16[768,512]{1,0:T(8,128)(2,1)S(1)}, bf16[768,512]{1,0:T(8,128)(2,1)S(1)}) custom-call(s32[4]{0:T(128)S(1)} %pad_add_fusion.place, f32[4,2048]{1,0:T(4,128)S(1)} %get-tuple-element.65.decay_ref, bf16[512,512]{1,0:T(8,128)(2,1)S(1)} %get-tuple-element.88.query_ref, ...), custom_call_target="tpu_custom_call" | custom-call | tf_op jit(solution)/shard_map/pallas_call | solution.py:44
  22.7 2.3 %collective-permute-done.4.other_ref = bf16[768,512]{1,0:T(8,128)(2,1)S(1)} collective-permute-done((bf16[768,512]{1,0:T(8,128)(2,1)S(1)}, bf16[768,512]{1,0:T(8,128)(2,1)S(1)}, u32[]{:S(2)}, u32[]{:S(2)}) %collective-permute-start.4) | collective-permute-done | bytes 786464 | tf_op jit(solution)/shard_map/ppermute | solution.py:354
  25.7 4.3 %collective-permute-start.5 = (bf16[2,192,256]{2,1,0:T(8,128)(2,1)S(1)}, bf16[2,192,256]{2,1,0:T(8,128)(2,1)S(1)}, u32[]{:S(2)}, u32[]{:S(2)}) collective-permute-start(bf16[2,192,256]{2,1,0:T(8,128)(2,1)S(1)} %get-tuple-element.76), channel_id=1, source_target_pairs={{0,2},{2,0},{4,6},{6,4},{1,3},{3,1},{5,7},{7,5},{8,10},{10,8},{12,... | collective-permute-start | bytes 589832 | tf_op jit(solution)/shard_map/ppermute | solution.py:354
  30.0 1.5 %shard_map.97.refs_0_ = f32[512,512]{1,0:T(8,128)S(1)} custom-call(s32[4]{0:T(128)S(1)} %pad_add_fusion.place, bf16[512,1536]{1,0:T(8,128)(2,1)S(1)} %bitcast.14, bf16[512,3072]{1,0:T(8,128)(2,1)S(1)} %copy-done), custom_call_target="tpu_custom_call" | custom-call | tf_op jit(solution)/shard_map/pallas_call | solution.py:44
  31.6 3.6 %collective-permute-done.5.other_ref = bf16[2,192,256]{2,1,0:T(8,128)(2,1)S(1)} collective-permute-done((bf16[2,192,256]{2,1,0:T(8,128)(2,1)S(1)}, bf16[2,192,256]{2,1,0:T(8,128)(2,1)S(1)}, u32[]{:S(2)}, u32[]{:S(2)}) %collective-permute-start.5) | collective-permute-done | bytes 196640 | tf_op jit(solution)/shard_map/ppermute | solution.py:354
  35.2 3.0 %collective-permute-done.grad_ref = bf16[512,1536]{1,0:T(8,128)(2,1)S(1)} collective-permute-done((bf16[512,1536]{1,0:T(8,128)(2,1)}, bf16[512,1536]{1,0:T(8,128)(2,1)S(1)}, u32[]{:S(2)}, u32[]{:S(2)}) %collective-permute-start) | collective-permute-done | bytes 1572896 | tf_op jit(solution)/shard_map/ppermute | solution.py:354
  41.3 1.3 %collective-permute-start.9 = (bf16[768,256]{1,0:T(8,128)(2,1)S(1)}, bf16[768,256]{1,0:T(8,128)(2,1)S(1)}, u32[]{:S(2)}, u32[]{:S(2)}) collective-permute-start(bf16[768,256]{1,0:T(8,128)(2,1)S(1)} %get-tuple-element.96), channel_id=1, source_target_pairs={{16,0},{24,8},{1,17},{9,25},{18,2},{26,10},{3,19},{11,27},{20,4},{... | collective-permute-start | bytes 1179656 | tf_op jit(solution)/shard_map/ppermute | solution.py:350
  42.7 4.6 %collective-permute-start.10 = (bf16[768,256]{1,0:T(8,128)(2,1)S(1)}, bf16[768,256]{1,0:T(8,128)(2,1)S(1)}, u32[]{:S(2)}, u32[]{:S(2)}) collective-permute-start(bf16[768,256]{1,0:T(8,128)(2,1)S(1)} %get-tuple-element.98), channel_id=1, source_target_pairs={{0,16},{8,24},{17,1},{25,9},{2,18},{10,26},{19,3},{27,11},{4,20},{... | collective-permute-start | bytes 1179656 | tf_op jit(solution)/shard_map/ppermute | solution.py:350
  47.9 1.9 %shard_map.103 = (bf16[512,512]{1,0:T(8,128)(2,1)S(1)}, bf16[4,128,128]{2,1,0:T(8,128)(2,1)S(1)}) custom-call(s32[4]{0:T(128)S(1)} %pad_add_fusion.place, bf16[512,1536]{1,0:T(8,128)(2,1)S(1)} %collective-permute-done.grad_ref, bf16[512,3072]{1,0:T(8,128)(2,1)S(1)} %copy-done, bf16[512,512]{1,0:T(8,128)(2,1)S(1)} %get-tuple-element.88.query_ref, ...), custom_call_target="tpu_custom_call" | custom-call | tf_op jit(solution)/shard_map/pallas_call | solution.py:44
  50.7 1.9 %collective-permute-start.11 = (bf16[2,192,256]{2,1,0:T(8,128)(2,1)S(1)}, bf16[2,192,256]{2,1,0:T(8,128)(2,1)S(1)}, u32[]{:S(2)}, u32[]{:S(2)}) collective-permute-start(bf16[2,192,256]{2,1,0:T(8,128)(2,1)S(1)} %get-tuple-element.101), channel_id=1, source_target_pairs={{0,2},{2,0},{4,6},{6,4},{1,3},{3,1},{5,7},{7,5},{8,10},{10,8},{12,... | collective-permute-start | bytes 589832 | tf_op jit(solution)/shard_map/ppermute | solution.py:354
  52.5 4.1 %shard_map.104 = (bf16[512,512]{1,0:T(8,128)(2,1)}, f32[512,512]{1,0:T(8,128)S(1)}, f32[512,512]{1,0:T(8,128)S(1)}) custom-call(bf16[512,512]{1,0:T(8,128)(2,1)S(1)} %get-tuple-element.88.query_ref, bf16[512,512]{1,0:T(8,128)(2,1)S(1)} %get-tuple-element.63.key_ref, bf16[512,512]{1,0:T(8,128)(2,1)S(1)} %get-tuple-element.64.value_ref, ...), custom_call_target="tpu_custom_call" | custom-call | tf_op jit(solution)/shard_map/pallas_call | solution.py:44
  59.5 4.3 %collective-permute-start.8 = (bf16[192,256]{1,0:T(8,128)(2,1)S(1)}, bf16[192,256]{1,0:T(8,128)(2,1)S(1)}, u32[]{:S(2)}, u32[]{:S(2)}) collective-permute-start(bf16[192,256]{1,0:T(8,128)(2,1)S(1)} %get-tuple-element.94), channel_id=1, source_target_pairs={{0,4},{2,6},{4,0},{6,2},{1,5},{3,7},{5,1},{7,3},{8,12},{10,14},{12... | collective-permute-start | bytes 294920 | tf_op jit(solution)/shard_map/ppermute | solution.py:354
  64.9 1.3 %collective-permute-start.16 = (bf16[4,128,128]{2,1,0:T(8,128)(2,1)S(1)}, bf16[4,128,128]{2,1,0:T(8,128)(2,1)S(1)}, u32[]{:S(2)}, u32[]{:S(2)}) collective-permute-start(bf16[4,128,128]{2,1,0:T(8,128)(2,1)S(1)} %shard_map.110), channel_id=1, source_target_pairs={{2,0},{3,1},{10,8},{11,9},{18,16},{19,17},{26,24},{27,25}} | collective-permute-start | bytes 393224 | tf_op jit(solution)/shard_map/ppermute | solution.py:481
  66.2 7.4 %collective-permute-done.8.own_other_ref = bf16[192,256]{1,0:T(8,128)(2,1)S(1)} collective-permute-done((bf16[192,256]{1,0:T(8,128)(2,1)S(1)}, bf16[192,256]{1,0:T(8,128)(2,1)S(1)}, u32[]{:S(2)}, u32[]{:S(2)}) %collective-permute-start.8) | collective-permute-done | bytes 98336 | tf_op jit(solution)/shard_map/ppermute | solution.py:354
  75.2 1.4 %collective-permute-start.17 = (bf16[192,256]{1,0:T(8,128)(2,1)S(1)}, bf16[192,256]{1,0:T(8,128)(2,1)S(1)}, u32[]{:S(2)}, u32[]{:S(2)}) collective-permute-start(bf16[192,256]{1,0:T(8,128)(2,1)S(1)} %get-tuple-element.117), channel_id=1, source_target_pairs={{0,16},{8,24},{16,0},{24,8},{1,17},{9,25},{17,1},{25,9},{2,18},{10... | collective-permute-start | bytes 294920 | tf_op jit(solution)/shard_map/ppermute | solution.py:354
  77.7 2.4 %shard_map.111 = (bf16[512,512]{1,0:T(8,128)(2,1)}, bf16[512,512]{1,0:T(8,128)(2,1)}) custom-call(s32[4]{0:T(128)S(1)} %pad_add_fusion.place, f32[4,2048]{1,0:T(4,128)S(1)} %get-tuple-element.65.decay_ref, bf16[512,512]{1,0:T(8,128)(2,1)S(1)} %get-tuple-element.63.key_ref, bf16[512,512]{1,0:T(8,128)(2,1)S(1)} %get-tuple-element.64.value_ref, ...), custom_call_target="tpu_custom_call" | custom-call | tf_op jit(solution)/shard_map/pallas_call | solution.py:44
  80.1 2.1 %collective-permute-done.18.later_other_ref = bf16[192,256]{1,0:T(8,128)(2,1)S(1)} collective-permute-done((bf16[192,256]{1,0:T(8,128)(2,1)S(1)}, bf16[192,256]{1,0:T(8,128)(2,1)S(1)}, u32[]{:S(2)}, u32[]{:S(2)}) %collective-permute-start.18) | collective-permute-done | bytes 98336 | tf_op jit(solution)/shard_map/ppermute | solution.py:354
  (39 shorter events, 14.3 us)
Async XLA Ops:
  0.6 37.7 %collective-permute-start = (bf16[512,1536]{1,0:T(8,128)(2,1)}, bf16[512,1536]{1,0:T(8,128)(2,1)S(1)}, u32[]{:S(2)}, u32[]{:S(2)}) collective-permute-start(bf16[512,1536]{1,0:T(8,128)(2,1)} %bitcast.12), channel_id=1, source_target_pairs={{0,1},{1,0},{2,3},{3,2},{4,5},{5,4},{6,7},{7,6},{8,9},{9,8},{10,11... | collective-permute-start | bytes 4718600 | tf_op jit(solution)/shard_map/ppermute | solution.py:354
  3.8 16.8 %copy-start.1 = (bf16[1,512,1536]{2,1,0:T(8,128)(2,1)S(1)}, bf16[1,512,1536]{2,1,0:T(8,128)(2,1)}, u32[]{:S(2)}) copy-start(bf16[1,512,1536]{2,1,0:T(8,128)(2,1)} %param.11) | copy-start | bytes 4718596
  6.9 11.0 %collective-permute-start.3 = (bf16[4,128,128]{2,1,0:T(8,128)(2,1)S(1)}, bf16[4,128,128]{2,1,0:T(8,128)(2,1)S(1)}, u32[]{:S(2)}, u32[]{:S(2)}) collective-permute-start(bf16[4,128,128]{2,1,0:T(8,128)(2,1)S(1)} %get-tuple-element.69), channel_id=1, source_target_pairs={{0,6},{1,7},{8,14},{9,15},{16,22},{17,23},{24,30},{25,31}} | collective-permute-start | bytes 393224 | tf_op jit(solution)/shard_map/ppermute | solution.py:335
  12.4 6.7 %collective-permute-start.2 = (bf16[4,128,128]{2,1,0:T(8,128)(2,1)S(1)}, bf16[4,128,128]{2,1,0:T(8,128)(2,1)S(1)}, u32[]{:S(2)}, u32[]{:S(2)}) collective-permute-start(bf16[4,128,128]{2,1,0:T(8,128)(2,1)S(1)} %get-tuple-element.69), channel_id=1, source_target_pairs={{0,4},{2,6},{1,5},{3,7},{8,12},{10,14},{9,13},{11,15},{16,20},{18,... | collective-permute-start | bytes 393224 | tf_op jit(solution)/shard_map/ppermute | solution.py:335
  13.7 6.8 %collective-permute-start.1 = (bf16[4,128,128]{2,1,0:T(8,128)(2,1)S(1)}, bf16[4,128,128]{2,1,0:T(8,128)(2,1)S(1)}, u32[]{:S(2)}, u32[]{:S(2)}) collective-permute-start(bf16[4,128,128]{2,1,0:T(8,128)(2,1)S(1)} %get-tuple-element.69), channel_id=1, source_target_pairs={{0,2},{2,4},{4,6},{1,3},{3,5},{5,7},{8,10},{10,12},{12,14},{9,11},... | collective-permute-start | bytes 393224 | tf_op jit(solution)/shard_map/ppermute | solution.py:335
  20.5 9.5 %copy-start = (bf16[512,3072]{1,0:T(8,128)(2,1)S(1)}, bf16[512,3072]{1,0:T(8,128)(2,1)}, u32[]{:S(2)}) copy-start(bf16[512,3072]{1,0:T(8,128)(2,1)} %out_ref.2) | copy-start | bytes 9437188
  22.6 2.4 %collective-permute-start.4 = (bf16[768,512]{1,0:T(8,128)(2,1)S(1)}, bf16[768,512]{1,0:T(8,128)(2,1)S(1)}, u32[]{:S(2)}, u32[]{:S(2)}) collective-permute-start(bf16[768,512]{1,0:T(8,128)(2,1)S(1)} %get-tuple-element.72), channel_id=1, source_target_pairs={{0,8},{8,0},{16,24},{24,16},{1,9},{9,1},{17,25},{25,17},{2,10},{10... | collective-permute-start | bytes 2359304 | tf_op jit(solution)/shard_map/ppermute | solution.py:354
  25.7 9.5 %collective-permute-start.5 = (bf16[2,192,256]{2,1,0:T(8,128)(2,1)S(1)}, bf16[2,192,256]{2,1,0:T(8,128)(2,1)S(1)}, u32[]{:S(2)}, u32[]{:S(2)}) collective-permute-start(bf16[2,192,256]{2,1,0:T(8,128)(2,1)S(1)} %get-tuple-element.76), channel_id=1, source_target_pairs={{0,2},{2,0},{4,6},{6,4},{1,3},{3,1},{5,7},{7,5},{8,10},{10,8},{12,... | collective-permute-start | bytes 589832 | tf_op jit(solution)/shard_map/ppermute | solution.py:354
  39.5 3.1 %collective-permute-start.6 = (bf16[768,256]{1,0:T(8,128)(2,1)S(1)}, bf16[768,256]{1,0:T(8,128)(2,1)S(1)}, u32[]{:S(2)}, u32[]{:S(2)}) collective-permute-start(bf16[768,256]{1,0:T(8,128)(2,1)S(1)} %get-tuple-element.83), channel_id=1, source_target_pairs={{0,8},{8,0},{16,24},{24,16},{1,9},{9,1},{17,25},{25,17},{2,10},{10... | collective-permute-start | bytes 1179656 | tf_op jit(solution)/shard_map/ppermute | solution.py:354
  40.7 6.6 %collective-permute-start.7 = (bf16[768,256]{1,0:T(8,128)(2,1)S(1)}, bf16[768,256]{1,0:T(8,128)(2,1)S(1)}, u32[]{:S(2)}, u32[]{:S(2)}) collective-permute-start(bf16[768,256]{1,0:T(8,128)(2,1)S(1)} %get-tuple-element.86), channel_id=1, source_target_pairs={{0,8},{8,0},{16,24},{24,16},{1,9},{9,1},{17,25},{25,17},{2,10},{10... | collective-permute-start | bytes 1179656 | tf_op jit(solution)/shard_map/ppermute | solution.py:354
  41.3 15.3 %collective-permute-start.9 = (bf16[768,256]{1,0:T(8,128)(2,1)S(1)}, bf16[768,256]{1,0:T(8,128)(2,1)S(1)}, u32[]{:S(2)}, u32[]{:S(2)}) collective-permute-start(bf16[768,256]{1,0:T(8,128)(2,1)S(1)} %get-tuple-element.96), channel_id=1, source_target_pairs={{16,0},{24,8},{1,17},{9,25},{18,2},{26,10},{3,19},{11,27},{20,4},{... | collective-permute-start | bytes 1179656 | tf_op jit(solution)/shard_map/ppermute | solution.py:350
  42.7 13.9 %collective-permute-start.10 = (bf16[768,256]{1,0:T(8,128)(2,1)S(1)}, bf16[768,256]{1,0:T(8,128)(2,1)S(1)}, u32[]{:S(2)}, u32[]{:S(2)}) collective-permute-start(bf16[768,256]{1,0:T(8,128)(2,1)S(1)} %get-tuple-element.98), channel_id=1, source_target_pairs={{0,16},{8,24},{17,1},{25,9},{2,18},{10,26},{19,3},{27,11},{4,20},{... | collective-permute-start | bytes 1179656 | tf_op jit(solution)/shard_map/ppermute | solution.py:350
  49.8 8.3 %collective-permute-start.14 = (bf16[4,128,128]{2,1,0:T(8,128)(2,1)S(1)}, bf16[4,128,128]{2,1,0:T(8,128)(2,1)S(1)}, u32[]{:S(2)}, u32[]{:S(2)}) collective-permute-start(bf16[4,128,128]{2,1,0:T(8,128)(2,1)S(1)} %get-tuple-element.113.back_ref), channel_id=1, source_target_pairs={{6,4},{7,5},{14,12},{15,13},{22,20},{23,21},{30,28},{31,29}} | collective-permute-start | bytes 393224 | tf_op jit(solution)/shard_map/ppermute | solution.py:481
  50.7 13.0 %collective-permute-start.11 = (bf16[2,192,256]{2,1,0:T(8,128)(2,1)S(1)}, bf16[2,192,256]{2,1,0:T(8,128)(2,1)S(1)}, u32[]{:S(2)}, u32[]{:S(2)}) collective-permute-start(bf16[2,192,256]{2,1,0:T(8,128)(2,1)S(1)} %get-tuple-element.101), channel_id=1, source_target_pairs={{0,2},{2,0},{4,6},{6,4},{1,3},{3,1},{5,7},{7,5},{8,10},{10,8},{12,... | collective-permute-start | bytes 589832 | tf_op jit(solution)/shard_map/ppermute | solution.py:354
  57.3 8.9 %collective-permute-start.12 = (bf16[2,192,256]{2,1,0:T(8,128)(2,1)S(1)}, bf16[2,192,256]{2,1,0:T(8,128)(2,1)S(1)}, u32[]{:S(2)}, u32[]{:S(2)}) collective-permute-start(bf16[2,192,256]{2,1,0:T(8,128)(2,1)S(1)} %get-tuple-element.104), channel_id=1, source_target_pairs={{0,2},{2,0},{4,6},{6,4},{1,3},{3,1},{5,7},{7,5},{8,10},{10,8},{12,... | collective-permute-start | bytes 589832 | tf_op jit(solution)/shard_map/ppermute | solution.py:354
  58.8 5.4 %collective-permute-start.15 = (bf16[4,128,128]{2,1,0:T(8,128)(2,1)S(1)}, bf16[4,128,128]{2,1,0:T(8,128)(2,1)S(1)}, u32[]{:S(2)}, u32[]{:S(2)}) collective-permute-start(bf16[4,128,128]{2,1,0:T(8,128)(2,1)S(1)} %shard_map.109), channel_id=1, source_target_pairs={{4,2},{5,3},{12,10},{13,11},{20,18},{21,19},{28,26},{29,27}} | collective-permute-start | bytes 393224 | tf_op jit(solution)/shard_map/ppermute | solution.py:481
  59.5 14.1 %collective-permute-start.8 = (bf16[192,256]{1,0:T(8,128)(2,1)S(1)}, bf16[192,256]{1,0:T(8,128)(2,1)S(1)}, u32[]{:S(2)}, u32[]{:S(2)}) collective-permute-start(bf16[192,256]{1,0:T(8,128)(2,1)S(1)} %get-tuple-element.94), channel_id=1, source_target_pairs={{0,4},{2,6},{4,0},{6,2},{1,5},{3,7},{5,1},{7,3},{8,12},{10,14},{12... | collective-permute-start | bytes 294920 | tf_op jit(solution)/shard_map/ppermute | solution.py:354
  63.8 10.9 %collective-permute-start.13 = (bf16[192,256]{1,0:T(8,128)(2,1)S(1)}, bf16[192,256]{1,0:T(8,128)(2,1)S(1)}, u32[]{:S(2)}, u32[]{:S(2)}) collective-permute-start(bf16[192,256]{1,0:T(8,128)(2,1)S(1)} %get-tuple-element.107), channel_id=1, source_target_pairs={{0,4},{2,6},{4,0},{6,2},{1,5},{3,7},{5,1},{7,3},{8,12},{10,14},{12... | collective-permute-start | bytes 294920 | tf_op jit(solution)/shard_map/ppermute | solution.py:354
  64.9 12.8 %collective-permute-start.16 = (bf16[4,128,128]{2,1,0:T(8,128)(2,1)S(1)}, bf16[4,128,128]{2,1,0:T(8,128)(2,1)S(1)}, u32[]{:S(2)}, u32[]{:S(2)}) collective-permute-start(bf16[4,128,128]{2,1,0:T(8,128)(2,1)S(1)} %shard_map.110), channel_id=1, source_target_pairs={{2,0},{3,1},{10,8},{11,9},{18,16},{19,17},{26,24},{27,25}} | collective-permute-start | bytes 393224 | tf_op jit(solution)/shard_map/ppermute | solution.py:481
  75.2 4.9 %collective-permute-start.17 = (bf16[192,256]{1,0:T(8,128)(2,1)S(1)}, bf16[192,256]{1,0:T(8,128)(2,1)S(1)}, u32[]{:S(2)}, u32[]{:S(2)}) collective-permute-start(bf16[192,256]{1,0:T(8,128)(2,1)S(1)} %get-tuple-element.117), channel_id=1, source_target_pairs={{0,16},{8,24},{16,0},{24,8},{1,17},{9,25},{17,1},{25,9},{2,18},{10... | collective-permute-start | bytes 294920 | tf_op jit(solution)/shard_map/ppermute | solution.py:354
  76.6 5.6 %collective-permute-start.18 = (bf16[192,256]{1,0:T(8,128)(2,1)S(1)}, bf16[192,256]{1,0:T(8,128)(2,1)S(1)}, u32[]{:S(2)}, u32[]{:S(2)}) collective-permute-start(bf16[192,256]{1,0:T(8,128)(2,1)S(1)} %get-tuple-element.118), channel_id=1, source_target_pairs={{0,4},{2,6},{4,0},{6,2},{1,5},{3,7},{5,1},{7,3},{8,12},{10,14},{12... | collective-permute-start | bytes 294920 | tf_op jit(solution)/shard_map/ppermute | solution.py:354

commit v3 on v2

--- a/solution.py
+++ b/solution.py
@@ -482,13 +482,6 @@
 
     returned = [pass_back(back, 1)] if paired else shift_down(back, seq_count)
     if paired:
-        grad_attn = after(grad_attn, back)
-    grad_queries, inner_keys, inner_values = call(
-        functools.partial(inner_kernel, heads=heads),
-        [final((rows, features), BF16), token_f32, token_f32],
-        [query, key, value, grad_attn, row, column, weight, carried],
-    )
-    if paired:
         def chain(stage, *behind):
             (passed,) = call(
                 functools.partial(chain_kernel, rows=rows),
@@ -498,18 +491,25 @@
             )
             return pass_back(passed, stage)
 
-        returned.append(chain(2, inner_keys))
+        far_stay, go = halve(far_stay, far_came, back)
+        far_came = swap(go, "seq", 2)
         later_stay, go = call(
             later_kernel,
             [shape((2, *later_part), F32), shape((2, *later_part), BF16)],
-            [own_later, own_later_came, after(later_stay, inner_keys), later_came],
+            [own_later, own_later_came, after(later_stay, far_stay), later_came],
             place,
         )
         later_came = swap(go, "seq", 1)
-        far_stay, go = halve(far_stay, far_came, later_stay)
-        far_came = swap(go, "seq", 2)
-        returned.append(chain(3, far_stay))
-        later_stay, go = halve(later_stay, later_came, far_stay)
+        returned.append(chain(2, later_stay))
+        grad_attn = after(grad_attn, later_stay)
+    grad_queries, inner_keys, inner_values = call(
+        functools.partial(inner_kernel, heads=heads),
+        [final((rows, features), BF16), token_f32, token_f32],
+        [query, key, value, grad_attn, row, column, weight, carried],
+    )
+    if paired:
+        returned.append(chain(3, inner_keys))
+        later_stay, go = halve(later_stay, later_came, inner_keys)
         later_came = swap(go, "seq", 2)
         first_keep, send = call(
             finish_kernel,

time: 83.2 us -> 83.2 us (level)
  waiting for transfers between devices: 23.2 us -> 21.2 us
  starting transfers between devices: 34.7 us -> 36.6 us
    ppermute x11, waiting for transfers between devices: 19.5 us -> 17.3 us  [swap(): lax.ppermute(value, axis, [(i, i ^ bit) for i in range(lax.axis_size(axis...]
    ppermute x11, starting transfers between devices: 16.8 us -> 18.7 us  [swap(): lax.ppermute(value, axis, [(i, i ^ bit) for i in range(lax.axis_size(axis...]
    ppermute x2, waiting for transfers between devices: 0.01 us -> 1.15 us  [to_chip(): return lax.ppermute(value, ('dp', 'tensor'), pairs)]
    ppermute x3, waiting for transfers between devices: 1.06 us -> 0.1 us  [pass_back(): lax.ppermute(value, 'seq', [(seq_count - stage, seq_count - 1 - stage)])]
  transfers between devices with their start and end apart: 19 -> 19, of which waited for: 9 -> 12; matrix products, arithmetic and copies ran while one was open for 0% -> 0% of each run, Pallas kernels for 27% -> 27%
where the time goes in v3:
time: 83.2 us; the launch traced here: 82.9 us
  starting transfers between devices  36.6 us (44%)
  Pallas kernels  24.1 us (29%)
  waiting for transfers between devices  21.2 us (25%)
  between operations  0.87 us (1%)
    pallas_call x20, Pallas kernels, call(): pl.pallas_call(body, out_shape=list(outs), grid_spec=spec, compiler_param...  24.1 us
    ppermute x11, starting transfers between devices, swap(): lax.ppermute(value, axis, [(i, i ^ bit) for i in range(lax.axis_size(axis...  18.7 us
    ppermute x11, waiting for transfers between devices, swap(): lax.ppermute(value, axis, [(i, i ^ bit) for i in range(lax.axis_size(axis...  17.3 us
    ppermute x3, starting transfers between devices, shift_up(): lax.ppermute(value, 'seq', [(i, i + k) for i in range(count - k)])  9.28 us
    ppermute x2, starting transfers between devices, to_chip(): return lax.ppermute(value, ('dp', 'tensor'), pairs)  5.87 us
    ppermute x3, starting transfers between devices, pass_back(): lax.ppermute(value, 'seq', [(seq_count - stage, seq_count - 1 - stage)])  2.81 us
    ppermute x3, waiting for transfers between devices, shift_up(): lax.ppermute(value, 'seq', [(i, i + k) for i in range(count - k)])  2.67 us
  transfers between devices with their start and end apart: 19, of which 12 were waited for; matrix products, arithmetic and copies ran while one was open for 0% of the time, Pallas kernels for 27%

profile of v3, /device:TPU:0, one launch (start us, length us, event | category | flops | bytes accessed | tf_op | source)
XLA Modules:
  0.0 82.9 jit_solution(15656314728059783525)
XLA Ops:
  0.6 3.1 %collective-permute-start = (bf16[512,1536]{1,0:T(8,128)(2,1)}, bf16[512,1536]{1,0:T(8,128)(2,1)S(1)}, u32[]{:S(2)}, u32[]{:S(2)}) collective-permute-start(bf16[512,1536]{1,0:T(8,128)(2,1)} %bitcast.12), channel_id=1, source_target_pairs={{0,1},{1,0},{2,3},{3,2},{4,5},{5,4},{6,7},{7,6},{8,9},{9,8},{10,11... | collective-permute-start | bytes 4718600 | tf_op jit(solution)/shard_map/ppermute | solution.py:354
  3.8 3.1 %shard_map.93 = (bf16[4,128,128]{2,1,0:T(8,128)(2,1)S(1)}, f32[8,512]{1,0:T(8,128)S(1)}, f32[512,8]{1,0:T(8,128)S(1)}, f32[4,2048]{1,0:T(4,128)S(1)}, bf16[512,5...) custom-call(s32[4]{0:T(128)S(1)} %pad_add_fusion.place, f32[4,2048]{1,0:T(4,128)} %bitcast.18, ...), custom_call_target="tpu_custom_call" | custom-call | tf_op jit(solution)/shard_map/pallas_call | solution.py:44
  6.9 5.5 %collective-permute-start.3 = (bf16[4,128,128]{2,1,0:T(8,128)(2,1)S(1)}, bf16[4,128,128]{2,1,0:T(8,128)(2,1)S(1)}, u32[]{:S(2)}, u32[]{:S(2)}) collective-permute-start(bf16[4,128,128]{2,1,0:T(8,128)(2,1)S(1)} %get-tuple-element.69), channel_id=1, source_target_pairs={{0,6},{1,7},{8,14},{9,15},{16,22},{17,23},{24,30},{25,31}} | collective-permute-start | bytes 393224 | tf_op jit(solution)/shard_map/ppermute | solution.py:335
  12.4 1.3 %collective-permute-start.2 = (bf16[4,128,128]{2,1,0:T(8,128)(2,1)S(1)}, bf16[4,128,128]{2,1,0:T(8,128)(2,1)S(1)}, u32[]{:S(2)}, u32[]{:S(2)}) collective-permute-start(bf16[4,128,128]{2,1,0:T(8,128)(2,1)S(1)} %get-tuple-element.69), channel_id=1, source_target_pairs={{0,4},{2,6},{1,5},{3,7},{8,12},{10,14},{9,13},{11,15},{16,20},{18,... | collective-permute-start | bytes 393224 | tf_op jit(solution)/shard_map/ppermute | solution.py:335
  13.7 2.5 %collective-permute-start.1 = (bf16[4,128,128]{2,1,0:T(8,128)(2,1)S(1)}, bf16[4,128,128]{2,1,0:T(8,128)(2,1)S(1)}, u32[]{:S(2)}, u32[]{:S(2)}) collective-permute-start(bf16[4,128,128]{2,1,0:T(8,128)(2,1)S(1)} %get-tuple-element.69), channel_id=1, source_target_pairs={{0,2},{2,4},{4,6},{1,3},{3,5},{5,7},{8,10},{10,12},{12,14},{9,11},... | collective-permute-start | bytes 393224 | tf_op jit(solution)/shard_map/ppermute | solution.py:335
  16.2 1.6 %shard_map.94 = (bf16[4,3,256,256]{3,2,1,0:T(8,128)(2,1)S(1)}, f32[512,512]{1,0:T(8,128)S(1)}) custom-call(bf16[512,512]{1,0:T(8,128)(2,1)S(1)} %get-tuple-element.88.query_ref, bf16[512,512]{1,0:T(8,128)(2,1)S(1)} %get-tuple-element.63.key_ref, bf16[512,512]{1,0:T(8,128)(2,1)S(1)} %get-tuple-element.64.value_ref, f32[8,512]{1,0:T(8,128)S(1)} %get-tuple-element.66.row_ref, ...), custom_call_target="tpu_custom_call" | custom-call | tf_op jit(solution)/shard_map/pallas_call | solution.py:44
  19.1 1.4 %collective-permute-done.1.refs_0_ = bf16[4,128,128]{2,1,0:T(8,128)(2,1)S(1)} collective-permute-done((bf16[4,128,128]{2,1,0:T(8,128)(2,1)S(1)}, bf16[4,128,128]{2,1,0:T(8,128)(2,1)S(1)}, u32[]{:S(2)}, u32[]{:S(2)}) %collective-permute-start.1) | collective-permute-done | bytes 131104 | tf_op jit(solution)/shard_map/ppermute | solution.py:335
  20.5 2.1 %shard_map.95 = (bf16[512,512]{1,0:T(8,128)(2,1)S(1)}, bf16[4,128,128]{2,1,0:T(8,128)(2,1)S(1)}, bf16[768,512]{1,0:T(8,128)(2,1)S(1)}, bf16[768,512]{1,0:T(8,128)(2,1)S(1)}) custom-call(s32[4]{0:T(128)S(1)} %pad_add_fusion.place, f32[4,2048]{1,0:T(4,128)S(1)} %get-tuple-element.65.decay_ref, bf16[512,512]{1,0:T(8,128)(2,1)S(1)} %get-tuple-element.88.query_ref, ...), custom_call_target="tpu_custom_call" | custom-call | tf_op jit(solution)/shard_map/pallas_call | solution.py:44
  22.7 2.3 %collective-permute-done.4.other_ref = bf16[768,512]{1,0:T(8,128)(2,1)S(1)} collective-permute-done((bf16[768,512]{1,0:T(8,128)(2,1)S(1)}, bf16[768,512]{1,0:T(8,128)(2,1)S(1)}, u32[]{:S(2)}, u32[]{:S(2)}) %collective-permute-start.4) | collective-permute-done | bytes 786464 | tf_op jit(solution)/shard_map/ppermute | solution.py:354
  25.7 4.3 %collective-permute-start.5 = (bf16[2,192,256]{2,1,0:T(8,128)(2,1)S(1)}, bf16[2,192,256]{2,1,0:T(8,128)(2,1)S(1)}, u32[]{:S(2)}, u32[]{:S(2)}) collective-permute-start(bf16[2,192,256]{2,1,0:T(8,128)(2,1)S(1)} %get-tuple-element.76), channel_id=1, source_target_pairs={{0,2},{2,0},{4,6},{6,4},{1,3},{3,1},{5,7},{7,5},{8,10},{10,8},{12,... | collective-permute-start | bytes 589832 | tf_op jit(solution)/shard_map/ppermute | solution.py:354
  30.0 1.5 %shard_map.97.refs_0_ = f32[512,512]{1,0:T(8,128)S(1)} custom-call(s32[4]{0:T(128)S(1)} %pad_add_fusion.place, bf16[512,1536]{1,0:T(8,128)(2,1)S(1)} %bitcast.14, bf16[512,3072]{1,0:T(8,128)(2,1)S(1)} %copy-done), custom_call_target="tpu_custom_call" | custom-call | tf_op jit(solution)/shard_map/pallas_call | solution.py:44
  31.6 3.6 %collective-permute-done.5.other_ref = bf16[2,192,256]{2,1,0:T(8,128)(2,1)S(1)} collective-permute-done((bf16[2,192,256]{2,1,0:T(8,128)(2,1)S(1)}, bf16[2,192,256]{2,1,0:T(8,128)(2,1)S(1)}, u32[]{:S(2)}, u32[]{:S(2)}) %collective-permute-start.5) | collective-permute-done | bytes 196640 | tf_op jit(solution)/shard_map/ppermute | solution.py:354
  35.2 3.0 %collective-permute-done.grad_ref = bf16[512,1536]{1,0:T(8,128)(2,1)S(1)} collective-permute-done((bf16[512,1536]{1,0:T(8,128)(2,1)}, bf16[512,1536]{1,0:T(8,128)(2,1)S(1)}, u32[]{:S(2)}, u32[]{:S(2)}) %collective-permute-start) | collective-permute-done | bytes 1572896 | tf_op jit(solution)/shard_map/ppermute | solution.py:354
  42.7 4.6 %collective-permute-start.10 = (bf16[768,256]{1,0:T(8,128)(2,1)S(1)}, bf16[768,256]{1,0:T(8,128)(2,1)S(1)}, u32[]{:S(2)}, u32[]{:S(2)}) collective-permute-start(bf16[768,256]{1,0:T(8,128)(2,1)S(1)} %get-tuple-element.97), channel_id=1, source_target_pairs={{0,16},{8,24},{17,1},{25,9},{2,18},{10,26},{19,3},{27,11},{4,20},{... | collective-permute-start | bytes 1179656 | tf_op jit(solution)/shard_map/ppermute | solution.py:350
  48.0 1.9 %collective-permute-start.9 = (bf16[2,192,256]{2,1,0:T(8,128)(2,1)S(1)}, bf16[2,192,256]{2,1,0:T(8,128)(2,1)S(1)}, u32[]{:S(2)}, u32[]{:S(2)}) collective-permute-start(bf16[2,192,256]{2,1,0:T(8,128)(2,1)S(1)} %get-tuple-element.94), channel_id=1, source_target_pairs={{0,2},{2,0},{4,6},{6,4},{1,3},{3,1},{5,7},{7,5},{8,10},{10,8},{12,... | collective-permute-start | bytes 589832 | tf_op jit(solution)/shard_map/ppermute | solution.py:354
  49.8 1.9 %shard_map.103 = (bf16[512,512]{1,0:T(8,128)(2,1)S(1)}, bf16[4,128,128]{2,1,0:T(8,128)(2,1)S(1)}) custom-call(s32[4]{0:T(128)S(1)} %pad_add_fusion.place, bf16[512,1536]{1,0:T(8,128)(2,1)S(1)} %collective-permute-done.grad_ref, bf16[512,3072]{1,0:T(8,128)(2,1)S(1)} %copy-done, bf16[512,512]{1,0:T(8,128)(2,1)S(1)} %get-tuple-element.88.query_ref, ...), custom_call_target="tpu_custom_call" | custom-call | tf_op jit(solution)/shard_map/pallas_call | solution.py:44
  52.4 2.0 %collective-permute-done.9.other_ref = bf16[2,192,256]{2,1,0:T(8,128)(2,1)S(1)} collective-permute-done((bf16[2,192,256]{2,1,0:T(8,128)(2,1)S(1)}, bf16[2,192,256]{2,1,0:T(8,128)(2,1)S(1)}, u32[]{:S(2)}, u32[]{:S(2)}) %collective-permute-start.9) | collective-permute-done | bytes 196640 | tf_op jit(solution)/shard_map/ppermute | solution.py:354
  56.2 1.9 %collective-permute-start.12 = (bf16[2,192,256]{2,1,0:T(8,128)(2,1)S(1)}, bf16[2,192,256]{2,1,0:T(8,128)(2,1)S(1)}, u32[]{:S(2)}, u32[]{:S(2)}) collective-permute-start(bf16[2,192,256]{2,1,0:T(8,128)(2,1)S(1)} %get-tuple-element.106), channel_id=1, source_target_pairs={{0,2},{2,0},{4,6},{6,4},{1,3},{3,1},{5,7},{7,5},{8,10},{10,8},{12,... | collective-permute-start | bytes 589832 | tf_op jit(solution)/shard_map/ppermute | solution.py:354
  59.7 4.3 %collective-permute-start.11 = (bf16[192,256]{1,0:T(8,128)(2,1)S(1)}, bf16[192,256]{1,0:T(8,128)(2,1)S(1)}, u32[]{:S(2)}, u32[]{:S(2)}) collective-permute-start(bf16[192,256]{1,0:T(8,128)(2,1)S(1)} %get-tuple-element.104), channel_id=1, source_target_pairs={{0,4},{2,6},{4,0},{6,2},{1,5},{3,7},{5,1},{7,3},{8,12},{10,14},{12... | collective-permute-start | bytes 294920 | tf_op jit(solution)/shard_map/ppermute | solution.py:354
  64.0 4.1 %shard_map.106 = (bf16[512,512]{1,0:T(8,128)(2,1)}, f32[512,512]{1,0:T(8,128)S(1)}, f32[512,512]{1,0:T(8,128)S(1)}) custom-call(bf16[512,512]{1,0:T(8,128)(2,1)S(1)} %get-tuple-element.88.query_ref, bf16[512,512]{1,0:T(8,128)(2,1)S(1)} %get-tuple-element.63.key_ref, bf16[512,512]{1,0:T(8,128)(2,1)S(1)} %get-tuple-element.64.value_ref, ...), custom_call_target="tpu_custom_call" | custom-call | tf_op jit(solution)/shard_map/pallas_call | solution.py:44
  70.1 2.3 %collective-permute-done.11.own_other_ref = bf16[192,256]{1,0:T(8,128)(2,1)S(1)} collective-permute-done((bf16[192,256]{1,0:T(8,128)(2,1)S(1)}, bf16[192,256]{1,0:T(8,128)(2,1)S(1)}, u32[]{:S(2)}, u32[]{:S(2)}) %collective-permute-start.11) | collective-permute-done | bytes 98336 | tf_op jit(solution)/shard_map/ppermute | solution.py:354
  74.1 2.5 %collective-permute-start.17 = (bf16[192,256]{1,0:T(8,128)(2,1)S(1)}, bf16[192,256]{1,0:T(8,128)(2,1)S(1)}, u32[]{:S(2)}, u32[]{:S(2)}) collective-permute-start(bf16[192,256]{1,0:T(8,128)(2,1)S(1)} %get-tuple-element.118), channel_id=1, source_target_pairs={{0,16},{8,24},{16,0},{24,8},{1,17},{9,25},{17,1},{25,9},{2,18},{10... | collective-permute-start | bytes 294920 | tf_op jit(solution)/shard_map/ppermute | solution.py:354
  76.7 2.4 %shard_map.111 = (bf16[512,512]{1,0:T(8,128)(2,1)}, bf16[512,512]{1,0:T(8,128)(2,1)}) custom-call(s32[4]{0:T(128)S(1)} %pad_add_fusion.place, f32[4,2048]{1,0:T(4,128)S(1)} %get-tuple-element.65.decay_ref, bf16[512,512]{1,0:T(8,128)(2,1)S(1)} %get-tuple-element.63.key_ref, bf16[512,512]{1,0:T(8,128)(2,1)S(1)} %get-tuple-element.64.value_ref, ...), custom_call_target="tpu_custom_call" | custom-call | tf_op jit(solution)/shard_map/pallas_call | solution.py:44
  79.2 2.9 %collective-permute-done.18.later_other_ref = bf16[192,256]{1,0:T(8,128)(2,1)S(1)} collective-permute-done((bf16[192,256]{1,0:T(8,128)(2,1)S(1)}, bf16[192,256]{1,0:T(8,128)(2,1)S(1)}, u32[]{:S(2)}, u32[]{:S(2)}) %collective-permute-start.18) | collective-permute-done | bytes 98336 | tf_op jit(solution)/shard_map/ppermute | solution.py:354
  (39 shorter events, 16.0 us)
Async XLA Ops:
  0.6 37.7 %collective-permute-start = (bf16[512,1536]{1,0:T(8,128)(2,1)}, bf16[512,1536]{1,0:T(8,128)(2,1)S(1)}, u32[]{:S(2)}, u32[]{:S(2)}) collective-permute-start(bf16[512,1536]{1,0:T(8,128)(2,1)} %bitcast.12), channel_id=1, source_target_pairs={{0,1},{1,0},{2,3},{3,2},{4,5},{5,4},{6,7},{7,6},{8,9},{9,8},{10,11... | collective-permute-start | bytes 4718600 | tf_op jit(solution)/shard_map/ppermute | solution.py:354
  3.8 16.8 %copy-start.1 = (bf16[1,512,1536]{2,1,0:T(8,128)(2,1)S(1)}, bf16[1,512,1536]{2,1,0:T(8,128)(2,1)}, u32[]{:S(2)}) copy-start(bf16[1,512,1536]{2,1,0:T(8,128)(2,1)} %param.11) | copy-start | bytes 4718596
  6.9 11.0 %collective-permute-start.3 = (bf16[4,128,128]{2,1,0:T(8,128)(2,1)S(1)}, bf16[4,128,128]{2,1,0:T(8,128)(2,1)S(1)}, u32[]{:S(2)}, u32[]{:S(2)}) collective-permute-start(bf16[4,128,128]{2,1,0:T(8,128)(2,1)S(1)} %get-tuple-element.69), channel_id=1, source_target_pairs={{0,6},{1,7},{8,14},{9,15},{16,22},{17,23},{24,30},{25,31}} | collective-permute-start | bytes 393224 | tf_op jit(solution)/shard_map/ppermute | solution.py:335
  12.4 6.7 %collective-permute-start.2 = (bf16[4,128,128]{2,1,0:T(8,128)(2,1)S(1)}, bf16[4,128,128]{2,1,0:T(8,128)(2,1)S(1)}, u32[]{:S(2)}, u32[]{:S(2)}) collective-permute-start(bf16[4,128,128]{2,1,0:T(8,128)(2,1)S(1)} %get-tuple-element.69), channel_id=1, source_target_pairs={{0,4},{2,6},{1,5},{3,7},{8,12},{10,14},{9,13},{11,15},{16,20},{18,... | collective-permute-start | bytes 393224 | tf_op jit(solution)/shard_map/ppermute | solution.py:335
  13.7 6.8 %collective-permute-start.1 = (bf16[4,128,128]{2,1,0:T(8,128)(2,1)S(1)}, bf16[4,128,128]{2,1,0:T(8,128)(2,1)S(1)}, u32[]{:S(2)}, u32[]{:S(2)}) collective-permute-start(bf16[4,128,128]{2,1,0:T(8,128)(2,1)S(1)} %get-tuple-element.69), channel_id=1, source_target_pairs={{0,2},{2,4},{4,6},{1,3},{3,5},{5,7},{8,10},{10,12},{12,14},{9,11},... | collective-permute-start | bytes 393224 | tf_op jit(solution)/shard_map/ppermute | solution.py:335
  20.5 9.5 %copy-start = (bf16[512,3072]{1,0:T(8,128)(2,1)S(1)}, bf16[512,3072]{1,0:T(8,128)(2,1)}, u32[]{:S(2)}) copy-start(bf16[512,3072]{1,0:T(8,128)(2,1)} %out_ref.2) | copy-start | bytes 9437188
  22.6 2.4 %collective-permute-start.4 = (bf16[768,512]{1,0:T(8,128)(2,1)S(1)}, bf16[768,512]{1,0:T(8,128)(2,1)S(1)}, u32[]{:S(2)}, u32[]{:S(2)}) collective-permute-start(bf16[768,512]{1,0:T(8,128)(2,1)S(1)} %get-tuple-element.72), channel_id=1, source_target_pairs={{0,8},{8,0},{16,24},{24,16},{1,9},{9,1},{17,25},{25,17},{2,10},{10... | collective-permute-start | bytes 2359304 | tf_op jit(solution)/shard_map/ppermute | solution.py:354
  25.7 9.5 %collective-permute-start.5 = (bf16[2,192,256]{2,1,0:T(8,128)(2,1)S(1)}, bf16[2,192,256]{2,1,0:T(8,128)(2,1)S(1)}, u32[]{:S(2)}, u32[]{:S(2)}) collective-permute-start(bf16[2,192,256]{2,1,0:T(8,128)(2,1)S(1)} %get-tuple-element.76), channel_id=1, source_target_pairs={{0,2},{2,0},{4,6},{6,4},{1,3},{3,1},{5,7},{7,5},{8,10},{10,8},{12,... | collective-permute-start | bytes 589832 | tf_op jit(solution)/shard_map/ppermute | solution.py:354
  39.5 3.1 %collective-permute-start.6 = (bf16[768,256]{1,0:T(8,128)(2,1)S(1)}, bf16[768,256]{1,0:T(8,128)(2,1)S(1)}, u32[]{:S(2)}, u32[]{:S(2)}) collective-permute-start(bf16[768,256]{1,0:T(8,128)(2,1)S(1)} %get-tuple-element.83), channel_id=1, source_target_pairs={{0,8},{8,0},{16,24},{24,16},{1,9},{9,1},{17,25},{25,17},{2,10},{10... | collective-permute-start | bytes 1179656 | tf_op jit(solution)/shard_map/ppermute | solution.py:354
  40.7 6.6 %collective-permute-start.7 = (bf16[768,256]{1,0:T(8,128)(2,1)S(1)}, bf16[768,256]{1,0:T(8,128)(2,1)S(1)}, u32[]{:S(2)}, u32[]{:S(2)}) collective-permute-start(bf16[768,256]{1,0:T(8,128)(2,1)S(1)} %get-tuple-element.86), channel_id=1, source_target_pairs={{0,8},{8,0},{16,24},{24,16},{1,9},{9,1},{17,25},{25,17},{2,10},{10... | collective-permute-start | bytes 1179656 | tf_op jit(solution)/shard_map/ppermute | solution.py:354
  41.3 13.1 %collective-permute-start.8 = (bf16[768,256]{1,0:T(8,128)(2,1)S(1)}, bf16[768,256]{1,0:T(8,128)(2,1)S(1)}, u32[]{:S(2)}, u32[]{:S(2)}) collective-permute-start(bf16[768,256]{1,0:T(8,128)(2,1)S(1)} %get-tuple-element.91), channel_id=1, source_target_pairs={{16,0},{24,8},{1,17},{9,25},{18,2},{26,10},{3,19},{11,27},{20,4},{... | collective-permute-start | bytes 1179656 | tf_op jit(solution)/shard_map/ppermute | solution.py:350
  42.7 12.8 %collective-permute-start.10 = (bf16[768,256]{1,0:T(8,128)(2,1)S(1)}, bf16[768,256]{1,0:T(8,128)(2,1)S(1)}, u32[]{:S(2)}, u32[]{:S(2)}) collective-permute-start(bf16[768,256]{1,0:T(8,128)(2,1)S(1)} %get-tuple-element.97), channel_id=1, source_target_pairs={{0,16},{8,24},{17,1},{25,9},{2,18},{10,26},{19,3},{27,11},{4,20},{... | collective-permute-start | bytes 1179656 | tf_op jit(solution)/shard_map/ppermute | solution.py:350
  48.0 6.4 %collective-permute-start.9 = (bf16[2,192,256]{2,1,0:T(8,128)(2,1)S(1)}, bf16[2,192,256]{2,1,0:T(8,128)(2,1)S(1)}, u32[]{:S(2)}, u32[]{:S(2)}) collective-permute-start(bf16[2,192,256]{2,1,0:T(8,128)(2,1)S(1)} %get-tuple-element.94), channel_id=1, source_target_pairs={{0,2},{2,0},{4,6},{6,4},{1,3},{3,1},{5,7},{7,5},{8,10},{10,8},{12,... | collective-permute-start | bytes 589832 | tf_op jit(solution)/shard_map/ppermute | solution.py:354
  51.7 6.4 %collective-permute-start.14 = (bf16[4,128,128]{2,1,0:T(8,128)(2,1)S(1)}, bf16[4,128,128]{2,1,0:T(8,128)(2,1)S(1)}, u32[]{:S(2)}, u32[]{:S(2)}) collective-permute-start(bf16[4,128,128]{2,1,0:T(8,128)(2,1)S(1)} %get-tuple-element.114.back_ref), channel_id=1, source_target_pairs={{6,4},{7,5},{14,12},{15,13},{22,20},{23,21},{30,28},{31,29}} | collective-permute-start | bytes 393224 | tf_op jit(solution)/shard_map/ppermute | solution.py:481
  56.2 13.8 %collective-permute-start.12 = (bf16[2,192,256]{2,1,0:T(8,128)(2,1)S(1)}, bf16[2,192,256]{2,1,0:T(8,128)(2,1)S(1)}, u32[]{:S(2)}, u32[]{:S(2)}) collective-permute-start(bf16[2,192,256]{2,1,0:T(8,128)(2,1)S(1)} %get-tuple-element.106), channel_id=1, source_target_pairs={{0,2},{2,0},{4,6},{6,4},{1,3},{3,1},{5,7},{7,5},{8,10},{10,8},{12,... | collective-permute-start | bytes 589832 | tf_op jit(solution)/shard_map/ppermute | solution.py:354
  58.8 9.2 %collective-permute-start.15 = (bf16[4,128,128]{2,1,0:T(8,128)(2,1)S(1)}, bf16[4,128,128]{2,1,0:T(8,128)(2,1)S(1)}, u32[]{:S(2)}, u32[]{:S(2)}) collective-permute-start(bf16[4,128,128]{2,1,0:T(8,128)(2,1)S(1)} %shard_map.109), channel_id=1, source_target_pairs={{4,2},{5,3},{12,10},{13,11},{20,18},{21,19},{28,26},{29,27}} | collective-permute-start | bytes 393224 | tf_op jit(solution)/shard_map/ppermute | solution.py:481
  59.7 12.8 %collective-permute-start.11 = (bf16[192,256]{1,0:T(8,128)(2,1)S(1)}, bf16[192,256]{1,0:T(8,128)(2,1)S(1)}, u32[]{:S(2)}, u32[]{:S(2)}) collective-permute-start(bf16[192,256]{1,0:T(8,128)(2,1)S(1)} %get-tuple-element.104), channel_id=1, source_target_pairs={{0,4},{2,6},{4,0},{6,2},{1,5},{3,7},{5,1},{7,3},{8,12},{10,14},{12... | collective-permute-start | bytes 294920 | tf_op jit(solution)/shard_map/ppermute | solution.py:354
  63.9 9.6 %collective-permute-start.13 = (bf16[192,256]{1,0:T(8,128)(2,1)S(1)}, bf16[192,256]{1,0:T(8,128)(2,1)S(1)}, u32[]{:S(2)}, u32[]{:S(2)}) collective-permute-start(bf16[192,256]{1,0:T(8,128)(2,1)S(1)} %get-tuple-element.109), channel_id=1, source_target_pairs={{0,4},{2,6},{4,0},{6,2},{1,5},{3,7},{5,1},{7,3},{8,12},{10,14},{12... | collective-permute-start | bytes 294920 | tf_op jit(solution)/shard_map/ppermute | solution.py:354
  68.7 8.0 %collective-permute-start.16 = (bf16[4,128,128]{2,1,0:T(8,128)(2,1)S(1)}, bf16[4,128,128]{2,1,0:T(8,128)(2,1)S(1)}, u32[]{:S(2)}, u32[]{:S(2)}) collective-permute-start(bf16[4,128,128]{2,1,0:T(8,128)(2,1)S(1)} %shard_map.110), channel_id=1, source_target_pairs={{2,0},{3,1},{10,8},{11,9},{18,16},{19,17},{26,24},{27,25}} | collective-permute-start | bytes 393224 | tf_op jit(solution)/shard_map/ppermute | solution.py:481
  74.1 5.1 %collective-permute-start.17 = (bf16[192,256]{1,0:T(8,128)(2,1)S(1)}, bf16[192,256]{1,0:T(8,128)(2,1)S(1)}, u32[]{:S(2)}, u32[]{:S(2)}) collective-permute-start(bf16[192,256]{1,0:T(8,128)(2,1)S(1)} %get-tuple-element.118), channel_id=1, source_target_pairs={{0,16},{8,24},{16,0},{24,8},{1,17},{9,25},{17,1},{25,9},{2,18},{10... | collective-permute-start | bytes 294920 | tf_op jit(solution)/shard_map/ppermute | solution.py:354
  76.6 5.5 %collective-permute-start.18 = (bf16[192,256]{1,0:T(8,128)(2,1)S(1)}, bf16[192,256]{1,0:T(8,128)(2,1)S(1)}, u32[]{:S(2)}, u32[]{:S(2)}) collective-permute-start(bf16[192,256]{1,0:T(8,128)(2,1)S(1)} %get-tuple-element.119), channel_id=1, source_target_pairs={{0,4},{2,6},{4,0},{6,2},{1,5},{3,7},{5,1},{7,3},{8,12},{10,14},{12... | collective-permute-start | bytes 294920 | tf_op jit(solution)/shard_map/ppermute | solution.py:354
